TPU v7x, 256 devices: a whole 4x4x8 slice. The times are simulated.
256 devices in a mesh: row: 16 (over z, core), col: 16 (over x, y).
Axes of the slice: x: 4, y: 4, z: 8, core: 2. Of those that a mesh axis runs over, the one named last changes fastest.
Arguments:
- targets: float32 [3, 131072], P(None, 'row'), may hold values from 0 to 1, as said below
- sources: float32 [3, 32768], P(None, 'col'), may hold values from 0 to 1, as said below
- samples: bfloat16 [32768, 128], P('col', 'row'), may hold values from -0.03125 to 0.03125
- near: int32 [256, 8], P('row'), may hold values from -1 to 63, as said below
Outputs:
- leaf_bases: float32 [131072, 128], P(('row', 'col'))
- nested: float32 [131072, 128], P(('row', 'col'))
Inputs may be any that keep to these rules, and one draw needn't show every extreme that they name: `near`: in each row, entries after the first -1 are -1 and the first entry is a source leaf; a row may name a source leaf twice. `targets`: the points of one leaf lie about a common centre. `sources`: the points of one leaf lie about a common centre.
All inputs are finite; a program needn't handle non-finite values.
Results may differ from a plain program's by a relative error of at most 0.0071.
Values may be sent and summed in bfloat16 or wider, within the bound.
No kernel may reach another device: no remote copies, remote signals or barrier semaphores. Data moves between devices by JAX's collectives and lax.ppermute only.
A program may use at most 64 MiB of HBM per device.

v0:
```python
import functools

import jax
import jax.numpy as jnp
from jax import lax
from jax.sharding import Mesh
from jax.sharding import PartitionSpec as P
from jax.experimental import pallas as pl
from jax.experimental.pallas import tpu as pltpu


LEAF = 512
corr_length = 0.1
ridge = 0.1
LOG2E = 1.4426950408889634
HI = lax.Precision.HIGHEST
F32 = jnp.float32
BF = jnp.bfloat16


def parts3(x):
    a = x.astype(BF).astype(F32)
    rest = x - a
    b = rest.astype(BF).astype(F32)
    return a, b, rest - b


def features(pts_ref, centre, source, masked=0.0):
    points = pts_ref[...]
    row = lax.broadcasted_iota(jnp.int32, points.shape, 0)
    shift = jnp.where(row < 3, (points - centre) * (LOG2E / corr_length), 0.0)
    norm = jnp.sum(shift * shift, axis=0, keepdims=True) + masked
    if source:
        a, b, c = parts3(jnp.where(row == 3, norm, jnp.where(row == 4, 1.0, shift)))
        stack = [a, b, a, c, b, a]
    else:
        a, b, c = parts3(jnp.where(row == 4, norm, jnp.where(row == 3, 1.0, -2.0 * shift)))
        stack = [a, a, b, a, b, c]
    return jnp.concatenate(stack, axis=0).astype(BF)


def kernel_tile(rows, cols):
    d2 = lax.dot_general(rows, cols, (((0,), (0,)), ((), ())), preferred_element_type=F32)
    d2 = jnp.maximum(d2, 1e-24)
    return jnp.exp2(-(d2 * lax.rsqrt(d2))).astype(BF)


def target_features(tgt_ref, pts_ref, row_leaf):
    pts_ref[...] = jnp.zeros_like(pts_ref)
    pts_ref[0:3, :] = tgt_ref[:, pl.ds(pl.multiple_of(row_leaf * LEAF, LEAF), LEAF)]
    centre = jnp.mean(pts_ref[...], axis=1, keepdims=True)
    return features(pts_ref, centre, False), centre


def place():
    return [lax.axis_index(a) for a in ("z", "c", "x", "y")]


def tile_of(q, i, leaf, near_ref, src_ref, pts_ref, cols, centre):
    _, c, x, y = place()
    chunk = jnp.bitwise_and(2 * c + i, 3)
    leaf_id = (jnp.bitwise_xor(x, q) * 4 + y) * 4 + chunk
    hit = near_ref[0, x * 4 + leaf] == leaf_id
    for k in range(1, 8):
        hit = jnp.logical_or(hit, near_ref[k, x * 4 + leaf] == leaf_id)
    pts_ref[0:3, :] = src_ref[:, pl.ds(pl.multiple_of(chunk * LEAF, LEAF), LEAF)]
    return kernel_tile(features(pts_ref, centre, True, jnp.where(hit, 1e9, 0.0)), cols)


def tiles_body(q, first, near_ref, tgt_ref, src_ref, out_ref, tpts_ref, spts_ref):
    _, _, x, y = place()
    spts_ref[...] = jnp.zeros_like(spts_ref)

    def one_leaf(turn, carry):
        leaf = jnp.bitwise_and(y + turn, 3)
        cols, centre = target_features(tgt_ref, tpts_ref, x * 4 + leaf)
        for i in range(4):
            out_ref[turn - first, i * LEAF:(i + 1) * LEAF, :] = tile_of(
                q, i, leaf, near_ref, src_ref, spts_ref.at[i], cols, centre)
        return carry

    lax.fori_loop(first, 4, one_leaf, 0)


def params():
    return pltpu.CompilerParams(vmem_limit_bytes=16 * 2**20)


def kernel_tiles(q, first, near, targets, sources):
    vm = pl.BlockSpec(memory_space=pltpu.VMEM)
    return pl.pallas_call(
        functools.partial(tiles_body, q, first),
        out_shape=jax.ShapeDtypeStruct((4 - first, 2048, LEAF), BF),
        in_specs=[pl.BlockSpec(memory_space=pltpu.SMEM), vm, vm],
        out_specs=vm,
        scratch_shapes=[pltpu.VMEM((8, LEAF), F32), pltpu.VMEM((4, 8, LEAF), F32)],
        cost_estimate=pl.CostEstimate(flops=8_000_000_000, bytes_accessed=8_400_000, transcendentals=8_400_000),
        compiler_params=params(),
        name="kernel_tiles",
    )(near, targets, sources)


def own_body(near_ref, tgt_ref, src_ref, mine_ref, other_ref, out_ref, held_ref, tpts_ref, spts_ref):
    _, _, x, y = place()
    spts_ref[...] = jnp.zeros_like(spts_ref)

    def one_leaf(turn, carry):
        leaf = jnp.bitwise_and(y + turn, 3)
        cols, centre = target_features(tgt_ref, tpts_ref, x * 4 + leaf)
        total = None
        for n, rows_ref in enumerate((mine_ref, other_ref)):
            for i in (2 * n, 2 * n + 1):
                held_ref[i * LEAF:(i + 1) * LEAF, :] = tile_of(
                    0, i, leaf, near_ref, src_ref, spts_ref.at[i], cols, centre)
            term = jnp.dot(rows_ref[...].reshape(128, 1024), held_ref[1024 * n:1024 * (n + 1), :], preferred_element_type=F32)
            total = term if total is None else total + term
        out_ref[turn] = total
        return carry

    lax.fori_loop(0, 4, one_leaf, 0)


def own_sums(near, targets, sources, mine, other):
    vm = pl.BlockSpec(memory_space=pltpu.VMEM)
    return pl.pallas_call(
        own_body,
        out_shape=jax.ShapeDtypeStruct((4, 128, LEAF), F32),
        in_specs=[pl.BlockSpec(memory_space=pltpu.SMEM)] + [vm] * 4,
        out_specs=vm,
        scratch_shapes=[pltpu.VMEM((2048, LEAF), BF), pltpu.VMEM((8, LEAF), F32), pltpu.VMEM((4, 8, LEAF), F32)],
        cost_estimate=pl.CostEstimate(flops=8_000_000_000, bytes_accessed=8_400_000, transcendentals=8_400_000),
        compiler_params=params(),
        name="own_sums",
    )(near, targets, sources, mine, other)


def sums_body(turn, stored, fused, near_ref, tgt_ref, base_ref, *refs):
    ns, nf = len(stored), len(fused)
    tiles, refs = refs[:ns], refs[ns:]
    srcs, refs = refs[:nf], refs[nf:]
    mine, refs = refs[:ns + nf], refs[ns + nf:]
    other, refs = refs[:ns + nf], refs[ns + nf:]
    out_ref, held_ref, tpts_ref, spts_ref = refs
    _, _, x, y = place()
    leaf = jnp.bitwise_and(y + turn, 3)
    cols, centre = target_features(tgt_ref, tpts_ref, x * 4 + leaf)
    spts_ref[...] = jnp.zeros_like(spts_ref)
    total = base_ref[turn]
    for n in range(ns + nf):
        rows = jnp.concatenate([mine[n][...].reshape(128, 1024), other[n][...].reshape(128, 1024)], axis=1)
        if n >= ns:
            for i in range(4):
                held_ref[n - ns, i * LEAF:(i + 1) * LEAF, :] = tile_of(
                    fused[n - ns], i, leaf, near_ref, srcs[n - ns], spts_ref.at[4 * (n - ns) + i], cols, centre)
            tile = held_ref[n - ns]
        else:
            tile = tiles[n][turn - 4 + tiles[n].shape[0]]
        total = total + jnp.dot(rows, tile, preferred_element_type=F32)
    out_ref[...] = total


def leaf_sums(turn, near, targets, base, tiles, sources, mine, other):
    stored, fused = sorted(tiles), sorted(sources)
    order = stored + fused
    vm = pl.BlockSpec(memory_space=pltpu.VMEM)
    sm = pl.BlockSpec(memory_space=pltpu.SMEM)
    return pl.pallas_call(
        functools.partial(sums_body, turn, stored, fused),
        out_shape=jax.ShapeDtypeStruct((128, LEAF), F32),
        in_specs=[sm, vm, vm] + [vm] * (3 * (len(stored) + len(fused))),
        scratch_shapes=[
            pltpu.VMEM((len(fused), 2048, LEAF), BF),
            pltpu.VMEM((8, LEAF), F32),
            pltpu.VMEM((4 * len(fused), 8, LEAF), F32),
        ],
        cost_estimate=pl.CostEstimate(flops=4_000_000_000, bytes_accessed=9_000_000, transcendentals=1_000_000),
        compiler_params=params(),
        name="leaf_sums",
    )(near, targets, base, *[tiles[q] for q in stored], *[sources[q] for q in fused],
      *[mine[q] for q in order], *[other[q] for q in order])


def eliminate(gram, aug_ref, top_ref):
    n = 128
    i = lax.broadcasted_iota(jnp.int32, (n, n), 0)
    j = lax.broadcasted_iota(jnp.int32, (n, n), 1)
    aug_ref[:, :n] = gram
    aug_ref[:, n:] = jnp.where(i == j, 1.0, 0.0)
    sub = lax.broadcasted_iota(jnp.int32, (8, n), 0)
    lane = lax.broadcasted_iota(jnp.int32, (8, n), 1)
    for b in range(n // 8):
        at = 8 * b
        left = aug_ref[at:at + 8, :n]
        right = aug_ref[at:at + 8, n:]
        cols = [jnp.broadcast_to(left[:, at + k:at + k + 1], (8, n)) for k in range(8)]
        scale = jnp.zeros((8, n), F32)
        for k in range(0, 8, 2):
            a = jnp.broadcast_to(cols[k][k:k + 1, :], (8, n))
            off = jnp.broadcast_to(cols[k + 1][k:k + 1, :], (8, n))
            d = jnp.broadcast_to(cols[k + 1][k + 1:k + 2, :], (8, n))
            inv = lax.rsqrt(a)
            rest = lax.rsqrt(a * d - off * off)
            scale = jnp.where(sub == k, inv, jnp.where(sub == k + 1, (a * inv) * rest, scale))
            for j, square in ((k, inv * inv), (k + 1, a * (rest * rest))):
                if j < 7:
                    mult = jnp.where(sub > j, cols[j] * square, 0.0)
                    for q in range(j + 1, 8):
                        cols[q] = cols[q] - mult * jnp.broadcast_to(cols[q][j:j + 1, :], (8, n))
                    left = left - mult * jnp.broadcast_to(left[j:j + 1, :], (8, n))
                    right = right - mult * jnp.broadcast_to(right[j:j + 1, :], (8, n))
        left = jnp.where(lane >= sub + at, left * scale, 0.0)
        right = right * scale
        top_ref[at:at + 8, :n] = left
        top_ref[at:at + 8, n:] = right
        if b < n // 8 - 1:
            l1, l2, l3 = parts3(left)
            r1, r2, r3 = parts3(right)
            lhs = jnp.concatenate([l1, l1, l2, l1, l2, l3], axis=0).astype(BF)
            rl = jnp.concatenate([l1, l2, l1, l3, l2, l1], axis=0)
            rr = jnp.concatenate([r1, r2, r1, r3, r2, r1], axis=0)
            rhs = jnp.concatenate([rl, rr], axis=1).astype(BF)
            upd = lax.dot_general(lhs, rhs, (((0,), (0,)), ((), ())), preferred_element_type=F32)
            aug_ref[at + 8:, :] -= upd[at + 8:, :]


def regular(gram):
    i = lax.broadcasted_iota(jnp.int32, gram.shape, 0)
    j = lax.broadcasted_iota(jnp.int32, gram.shape, 1)
    diag = jnp.where(i == j, gram, 0.0)
    mean = jnp.sum(jnp.sum(diag, axis=1, keepdims=True), axis=0, keepdims=True) / gram.shape[0]
    return gram / mean + jnp.where(i == j, ridge, 0.0), mean


def factors(gram, aug_ref, top_ref):
    scaled, mean = regular(gram)
    eliminate(scaled, aug_ref, top_ref)
    inv = top_ref[:, 128:]
    root = lax.rsqrt(mean)
    return inv * root, (top_ref[:, :128] - ridge * inv) * (mean * root)


def tdot(a, b):
    return lax.dot_general(a, b, (((0,), (0,)), ((), ())), precision=HI, preferred_element_type=F32)


def ndot(a, b):
    return lax.dot_general(a, b, (((1,), (1,)), ((), ())), precision=HI, preferred_element_type=F32)


def mdot(a, b):
    return lax.dot_general(a, b, (((1,), (0,)), ((), ())), precision=HI, preferred_element_type=F32)


def leaf_body(a_ref, b_ref, c_ref, d_ref, z_ref, inv_ref, proj_ref, sq_ref, aug_ref, top_ref):
    for k in range(4):
        for s in range(2):
            plane = jnp.bitwise_xor(jnp.bitwise_and(place()[0] - 2 * k, 7), s)
            rows = slice(16 * (2 * k + s), 16 * (2 * k + s) + 16)
            both = (a_ref[rows, :] + b_ref[rows, :]) + (c_ref[rows, :] + d_ref[rows, :])
            z_ref[pl.ds(pl.multiple_of(plane * 16, 16), 16), :] = both
    z = z_ref[...]
    inv, proj = factors(ndot(z, z) * (1.0 / LEAF), aug_ref, top_ref)
    inv_ref[...] = inv
    proj_ref[...] = proj
    sq_ref[...] = tdot(proj, proj)


def node_body(a_ref, b_ref, inv_ref, proj_ref, sq_ref, aug_ref, top_ref):
    inv, proj = factors((a_ref[...] + b_ref[...]) * (1.0 / 256), aug_ref, top_ref)
    inv_ref[...] = inv
    proj_ref[...] = proj
    sq_ref[...] = tdot(proj, proj)


def carry_body(z_ref, inv_ref, proj_ref, base_ref, next_ref):
    base = lax.dot_general(z_ref[...], inv_ref[...], (((0,), (1,)), ((), ())), precision=HI, preferred_element_type=F32)
    base_ref[...] = base
    next_ref[...] = mdot(base, proj_ref[...])


def carry2_body(z_ref, inv_ref, proj_ref, next_ref):
    next_ref[...] = mdot(ndot(z_ref[...], inv_ref[...]), proj_ref[...])


def last_body(a_ref, b_ref, z_ref, out_ref, aug_ref, top_ref):
    inv, _ = factors((a_ref[...] + b_ref[...]) * (1.0 / 256), aug_ref, top_ref)
    out_ref[...] = ndot(z_ref[...], inv) * (1.0 / 128)


def sds(*shape):
    return jax.ShapeDtypeStruct(shape, F32)


SCR = [pltpu.VMEM((128, 256), F32), pltpu.VMEM((128, 256), F32)]


def leaf_node(parts):
    vm = pl.BlockSpec(memory_space=pltpu.VMEM)
    return pl.pallas_call(
        leaf_body,
        out_shape=(sds(128, LEAF),) + (sds(128, 128),) * 3,
        in_specs=[vm] * 4,
        scratch_shapes=SCR,
        name="leaf_node",
        compiler_params=params(),
    )(*parts)


def pair_node(a, b):
    return pl.pallas_call(node_body, out_shape=(sds(128, 128),) * 3, scratch_shapes=SCR, name="pair_node", compiler_params=params())(a, b)


def carry(z, inv, proj):
    return pl.pallas_call(carry_body, out_shape=(sds(512, 128),) * 2, name="carry", compiler_params=params())(z, inv, proj)


def carry2(z, inv, proj):
    return pl.pallas_call(carry2_body, out_shape=sds(512, 128), name="carry2", compiler_params=params())(z, inv, proj)


def last_node(a, b, z):
    return pl.pallas_call(last_body, out_shape=sds(512, 128), scratch_shapes=SCR, name="last_node", compiler_params=params())(a, b, z)


ROW = ("z", "c")
COL = ("x", "y")


def moved(x, axis, by):
    size = lax.axis_size(axis)
    return lax.ppermute(x, axis, [(i, (i + by) % size) for i in range(size)])


def crossed(x, axis, bit):
    return lax.ppermute(x, axis, [(i, i ^ bit) for i in range(lax.axis_size(axis))])


def diagonal(x):
    return lax.ppermute(x, ROW, [(i, i ^ 3) for i in range(16)])


def own_pair(samples, core):
    flat = samples.T
    half = flat.shape[1] // 2
    mine = lax.dynamic_slice_in_dim(flat, core * half, half, 1)
    away = lax.dynamic_slice_in_dim(flat, (1 - core) * half, half, 1)
    across, up, cross = crossed(away, "c", 1), crossed(mine, "z", 1), diagonal(away)
    first = jnp.where(core == 0, jnp.concatenate([mine, across]), jnp.concatenate([across, mine]))
    second = jnp.where(core == 0, jnp.concatenate([up, cross]), jnp.concatenate([cross, up]))
    return jnp.concatenate([first, second])


def after(x, *work):
    return lax.optimization_barrier((x, *work))[0]


def per_device(targets, sources, samples, near):
    core = lax.axis_index("c")
    near = near.T
    beside = crossed(sources, "x", 1)
    pair = own_pair(samples, core)
    block = jnp.stack([pair] + [moved(pair, "z", 2 * k) for k in (1, 2, 3)])
    behind = crossed(jnp.stack([sources, beside]), "x", 2)
    tiles = {1: kernel_tiles(1, 0, near, targets, after(beside, pair))}
    block = after(block, tiles[1])
    sent = {q: crossed(block, "x", q) for q in (2, 1, 3)}
    swapped = crossed(block, "c", 1)
    tiles[3] = kernel_tiles(3, 1, near, targets, after(behind[1], swapped))
    base = own_sums(near, targets, sources, block, after(swapped, tiles[3]))
    mine = {q: after(b, base) for q, b in sent.items()}
    other = {q: crossed(b, "c", 1) for q, b in mine.items()}
    sums = {}
    for d in (2, 1, 3, 0):
        made = tiles if d else {1: tiles[1]}
        fused = {2: behind[0]} if d else {2: behind[0], 3: behind[1]}
        part = leaf_sums(d, near, targets, base, made, fused, mine, other)
        sums[d] = moved(part, "y", d) if d else part
    far_sample, inv0, proj0, sq0 = leaf_node([sums[d] for d in range(4)])
    sib = crossed(sq0, "y", 1)
    leaf_basis, carried = carry(far_sample, inv0, proj0)
    inv1, proj1, sq1 = pair_node(sq0, after(sib, carried))
    cousin = crossed(sq1, "y", 2)
    carried = carry2(carried, inv1, proj1)
    nested = last_node(sq1, cousin, carried)
    return (leaf_basis, nested)


def solution(mesh):
    torus = Mesh(mesh.devices.reshape(8, 2, 4, 4), ("z", "c", "x", "y"))
    return jax.shard_map(
        per_device,
        mesh=torus,
        in_specs=(P(None, ROW), P(None, COL), P(COL, ROW), P(ROW, None)),
        out_specs=(P(ROW + COL, None), P(ROW + COL, None)),
        check_vma=False,
    )
```

profile of v0, /device:TPU:8, one launch (start us, length us, event | category | flops | bytes accessed | tf_op | source)
XLA Modules:
  0.0 100.7 jit_solution(4774596484531027242)
XLA Ops:
  1.4 2.0 %collective-permute-start.2 = (bf16[8,1024]{1,0:T(8,128)(2,1)S(1)}, bf16[8,1024]{1,0:T(8,128)(2,1)S(1)}, u32[]{:S(2)}, u32[]{:S(2)}) collective-permute-start(bf16[8,1024]{1,0:T(8,128)(2,1)S(1)} %get-tuple-element.41), channel_id=1, source_target_pairs={{0,48},{16,32},{32,16},{48,0},{64,112},{80,96},{96,80},{112,64},{1... | collective-permute-start | bytes 49160 | tf_op jit(solution)/shard_map/ppermute | solution.py:339
  3.5 1.5 %collective-permute-start.6 = (f32[3,2048]{1,0:T(4,128)}, f32[3,2048]{1,0:T(4,128)S(1)}, u32[]{:S(2)}, u32[]{:S(2)}) collective-permute-start(f32[3,2048]{1,0:T(4,128)} %src_ref.1), channel_id=1, source_target_pairs={{0,4},{4,0},{8,12},{12,8},{1,5},{5,1},{9,13},{13,9},{2,6},{6,2},{1... | collective-permute-start | bytes 73736 | tf_op jit(solution)/shard_map/ppermute | solution.py:335
  5.0 2.1 %collective-permute-done.1 = bf16[8,1024]{1,0:T(8,128)(2,1)S(1)} collective-permute-done((bf16[8,1024]{1,0:T(8,128)(2,1)S(1)}, bf16[8,1024]{1,0:T(8,128)(2,1)S(1)}, u32[]{:S(2)}, u32[]{:S(2)}) %collective-permute-start.1) | collective-permute-done | bytes 16416 | tf_op jit(solution)/shard_map/ppermute | solution.py:335
  7.2 3.3 %collective-permute-start.3 = (bf16[32,1024]{1,0:T(8,128)(2,1)S(1)}, bf16[32,1024]{1,0:T(8,128)(2,1)S(1)}, u32[]{:S(2)}, u32[]{:S(2)}) collective-permute-start(bf16[32,1024]{1,0:T(8,128)(2,1)S(1)} %get-tuple-element.39), channel_id=1, source_target_pairs={{0,64},{32,96},{64,128},{96,160},{128,192},{160,224},{192,0},{224,... | collective-permute-start | bytes 196616 | tf_op jit(solution)/shard_map/ppermute | solution.py:331
  10.5 4.5 %collective-permute-start.4 = (bf16[32,1024]{1,0:T(8,128)(2,1)S(1)}, bf16[32,1024]{1,0:T(8,128)(2,1)S(1)}, u32[]{:S(2)}, u32[]{:S(2)}) collective-permute-start(bf16[32,1024]{1,0:T(8,128)(2,1)S(1)} %get-tuple-element.39), channel_id=1, source_target_pairs={{0,128},{32,160},{64,192},{96,224},{128,0},{160,32},{192,64},{224,... | collective-permute-start | bytes 196616 | tf_op jit(solution)/shard_map/ppermute | solution.py:331
  15.0 2.7 %collective-permute-start.5 = (bf16[32,1024]{1,0:T(8,128)(2,1)S(1)}, bf16[32,1024]{1,0:T(8,128)(2,1)S(1)}, u32[]{:S(2)}, u32[]{:S(2)}) collective-permute-start(bf16[32,1024]{1,0:T(8,128)(2,1)S(1)} %get-tuple-element.39), channel_id=1, source_target_pairs={{0,192},{32,224},{64,0},{96,32},{128,64},{160,96},{192,128},{224,1... | collective-permute-start | bytes 196616 | tf_op jit(solution)/shard_map/ppermute | solution.py:331
  17.7 0.8 pad_maximum_fusion.2
  18.5 3.1 %collective-permute-start.8 = (f32[2,3,2048]{2,1,0:T(4,128)S(1)}, f32[2,3,2048]{2,1,0:T(4,128)S(1)}, u32[]{:S(2)}, u32[]{:S(2)}) collective-permute-start(f32[2,3,2048]{2,1,0:T(4,128)S(1)} %pad_maximum_fusion.2), channel_id=1, source_target_pairs={{0,8},{4,12},{8,0},{12,4},{1,9},{5,13},{9,1},{13,5},{2,10},{6,14},... | collective-permute-start | bytes 147464 | tf_op jit(solution)/shard_map/ppermute | solution.py:335
  21.6 0.9 copy-done
  23.2 6.2 %kernel_tiles.2.refs_0_ = bf16[4,2048,512]{2,1,0:T(8,128)(2,1)S(1)} custom-call(s32[8,16]{1,0:T(8,128)S(1)} %bitcast.16, f32[3,8192]{1,0:T(4,128)S(1)} %copy-done, f32[3,2048]{1,0:T(4,128)S(1)} %collective-permute-done.6.src_ref), custom_call_target="tpu_custom_call" | custom-call | flops 8000000000 | bytes 8400000 | tf_op jit(solution)/shard_map/kernel_tiles/pallas_call | solution.py:91
  29.6 1.2 %collective-permute-start.11 = (bf16[4,32,1024]{2,1,0:T(8,128)(2,1)S(1)}, bf16[4,32,1024]{2,1,0:T(8,128)(2,1)S(1)}, u32[]{:S(2)}, u32[]{:S(2)}) collective-permute-start(bf16[4,32,1024]{2,1,0:T(8,128)(2,1)S(1)} %pad_maximum_fusion.mine_ref), channel_id=1, source_target_pairs={{0,12},{4,8},{8,4},{12,0},{1,13},{5,9},{9,5},{13,1},{2,14},{6,10},... | collective-permute-start | bytes 786440 | tf_op jit(solution)/shard_map/ppermute | solution.py:335
  30.9 1.5 %collective-permute-start.10 = (bf16[4,32,1024]{2,1,0:T(8,128)(2,1)S(1)}, bf16[4,32,1024]{2,1,0:T(8,128)(2,1)S(1)}, u32[]{:S(2)}, u32[]{:S(2)}) collective-permute-start(bf16[4,32,1024]{2,1,0:T(8,128)(2,1)S(1)} %pad_maximum_fusion.mine_ref), channel_id=1, source_target_pairs={{0,8},{4,12},{8,0},{12,4},{1,9},{5,13},{9,1},{13,5},{2,10},{6,14},... | collective-permute-start | bytes 786440 | tf_op jit(solution)/shard_map/ppermute | solution.py:335
  32.4 1.4 %collective-permute-start.9 = (bf16[4,32,1024]{2,1,0:T(8,128)(2,1)S(1)}, bf16[4,32,1024]{2,1,0:T(8,128)(2,1)S(1)}, u32[]{:S(2)}, u32[]{:S(2)}) collective-permute-start(bf16[4,32,1024]{2,1,0:T(8,128)(2,1)S(1)} %pad_maximum_fusion.mine_ref), channel_id=1, source_target_pairs={{0,4},{4,0},{8,12},{12,8},{1,5},{5,1},{9,13},{13,9},{2,6},{6,2},{1... | collective-permute-start | bytes 786440 | tf_op jit(solution)/shard_map/ppermute | solution.py:335
  33.8 4.8 %kernel_tiles.3.refs_1_ = bf16[3,2048,512]{2,1,0:T(8,128)(2,1)S(1)} custom-call(s32[8,16]{1,0:T(8,128)S(1)} %bitcast.17, f32[3,8192]{1,0:T(4,128)S(1)} %copy-done, f32[3,2048]{1,0:T(4,128)S(1)} %get-tuple-element.21.src_ref.refs_2_), custom_call_target="tpu_custom_call" | custom-call | flops 8000000000 | bytes 8400000 | tf_op jit(solution)/shard_map/kernel_tiles/pallas_call | solution.py:91
  38.7 7.8 %own_sums.1.base_ref = f32[4,128,512]{2,1,0:T(8,128)S(1)} custom-call(s32[8,16]{1,0:T(8,128)S(1)} %bitcast.18, f32[3,8192]{1,0:T(4,128)S(1)} %copy-done, f32[3,2048]{1,0:T(4,128)S(1)} %copy-done.2, bf16[4,32,1024]{2,1,0:T(8,128)(2,1)S(1)} %pad_maximum_fusion.mine_ref, bf16[4,32,1024]{2,1,0:T(8,128)(2,1)S(1)} %collective-permute-done.7.other_ref), custom_call_target="tpu_custom_call" | custom-call | flops 8000000000 | bytes 8400000 | tf_op jit(solution)/shard_map/own_sums/pallas_call | solution.py:125
  47.3 0.9 collective-permute-done.14.refs_8_.refs_7_
  49.0 2.7 %leaf_sums.7 = f32[128,512]{1,0:T(8,128)S(1)} custom-call(s32[8,16]{1,0:T(8,128)S(1)} %bitcast.19, f32[3,8192]{1,0:T(4,128)S(1)} %copy-done, f32[4,128,512]{2,1,0:T(8,128)S(1)} %own_sums.1.base_ref, bf16[4,2048,512]{2,1,0:T(8,128)(2,1)S(1)} %kernel_tiles.2.refs_0_, bf16[3,2048,512]{2,1,0:T(8,128)(2,1)S(1)} %kernel_tiles.3.refs_1_, ...), custom_call_target="tpu_custom_call" | custom-call | flops 4000000000 | bytes 9000000 | tf_op jit(solution)/shard_map/leaf_sums/pallas_call | solution.py:167
  52.3 2.7 %leaf_sums.6 = f32[128,512]{1,0:T(8,128)S(1)} custom-call(s32[8,16]{1,0:T(8,128)S(1)} %bitcast.20, f32[3,8192]{1,0:T(4,128)S(1)} %copy-done, f32[4,128,512]{2,1,0:T(8,128)S(1)} %own_sums.1.base_ref, bf16[4,2048,512]{2,1,0:T(8,128)(2,1)S(1)} %kernel_tiles.2.refs_0_, bf16[3,2048,512]{2,1,0:T(8,128)(2,1)S(1)} %kernel_tiles.3.refs_1_, ...), custom_call_target="tpu_custom_call" | custom-call | flops 4000000000 | bytes 9000000 | tf_op jit(solution)/shard_map/leaf_sums/pallas_call | solution.py:167
  55.0 2.7 %collective-permute-start.16 = (f32[128,512]{1,0:T(8,128)S(1)}, f32[128,512]{1,0:T(8,128)S(1)}, u32[]{:S(2)}, u32[]{:S(2)}) collective-permute-start(f32[128,512]{1,0:T(8,128)S(1)} %leaf_sums.6), channel_id=1, source_target_pairs={{0,2},{1,3},{2,0},{3,1},{4,6},{5,7},{6,4},{7,5},{8,10},{9,11},{10,... | collective-permute-start | bytes 786440 | tf_op jit(solution)/shard_map/ppermute | solution.py:331
  57.6 2.7 %leaf_sums.5 = f32[128,512]{1,0:T(8,128)S(1)} custom-call(s32[8,16]{1,0:T(8,128)S(1)} %bitcast.21, f32[3,8192]{1,0:T(4,128)S(1)} %copy-done, f32[4,128,512]{2,1,0:T(8,128)S(1)} %own_sums.1.base_ref, bf16[4,2048,512]{2,1,0:T(8,128)(2,1)S(1)} %kernel_tiles.2.refs_0_, bf16[3,2048,512]{2,1,0:T(8,128)(2,1)S(1)} %kernel_tiles.3.refs_1_, ...), custom_call_target="tpu_custom_call" | custom-call | flops 4000000000 | bytes 9000000 | tf_op jit(solution)/shard_map/leaf_sums/pallas_call | solution.py:167
  60.4 2.2 %collective-permute-start.15 = (f32[128,512]{1,0:T(8,128)S(1)}, f32[128,512]{1,0:T(8,128)S(1)}, u32[]{:S(2)}, u32[]{:S(2)}) collective-permute-start(f32[128,512]{1,0:T(8,128)S(1)} %leaf_sums.5), channel_id=1, source_target_pairs={{0,1},{1,2},{2,3},{3,0},{4,5},{5,6},{6,7},{7,4},{8,9},{9,10},{10,1... | collective-permute-start | bytes 786440 | tf_op jit(solution)/shard_map/ppermute | solution.py:331
  62.6 3.9 %leaf_sums.4.a_ref = f32[128,512]{1,0:T(8,128)S(1)} custom-call(s32[8,16]{1,0:T(8,128)S(1)} %bitcast.22, f32[3,8192]{1,0:T(4,128)S(1)} %copy-done, f32[4,128,512]{2,1,0:T(8,128)S(1)} %own_sums.1.base_ref, bf16[4,2048,512]{2,1,0:T(8,128)(2,1)S(1)} %kernel_tiles.2.refs_0_, f32[3,2048]{1,0:T(4,128)S(1)} %get-tuple-element.36.refs_1_.refs_2_, ...), custom_call_target="tpu_custom_call" | custom-call | flops 4000000000 | bytes 9000000 | tf_op jit(solution)/shard_map/leaf_sums/pallas_call | solution.py:167
  66.8 3.6 %collective-permute-done.15.b_ref = f32[128,512]{1,0:T(8,128)S(1)} collective-permute-done((f32[128,512]{1,0:T(8,128)S(1)}, f32[128,512]{1,0:T(8,128)S(1)}, u32[]{:S(2)}, u32[]{:S(2)}) %collective-permute-start.15) | collective-permute-done | bytes 262176 | tf_op jit(solution)/shard_map/ppermute | solution.py:331
  70.4 6.4 %leaf_node.1 = (f32[128,512]{1,0:T(8,128)S(1)}, f32[128,128]{1,0:T(8,128)S(1)}, f32[128,128]{1,0:T(8,128)S(1)}, f32[128,128]{1,0:T(8,128)S(1)}) custom-call(f32[128,512]{1,0:T(8,128)S(1)} %leaf_sums.4.a_ref, f32[128,512]{1,0:T(8,128)S(1)} %collective-permute-done.15.b_ref, f32[128,512]{1,0:T(8,128)S(1)} %collective-permute-done.16.c_ref, ...), custom_call_target="tpu_custom_call" | custom-call | tf_op jit(solution)/shard_map/leaf_node/pallas_call | solution.py:299
  76.8 3.0 %collective-permute-start.18 = (f32[128,128]{1,0:T(8,128)S(1)}, f32[128,128]{1,0:T(8,128)S(1)}, u32[]{:S(2)}, u32[]{:S(2)}) collective-permute-start(f32[128,128]{1,0:T(8,128)S(1)} %get-tuple-element.30.a_ref), channel_id=1, source_target_pairs={{0,1},{1,0},{2,3},{3,2},{4,5},{5,4},{6,7},{7,6},{8,9},{9,8},{10,11... | collective-permute-start | bytes 196616 | tf_op jit(solution)/shard_map/ppermute | solution.py:335
  79.8 1.3 %carry.1 = (f32[512,128]{1,0:T(8,128)}, f32[512,128]{1,0:T(8,128)S(1)}) custom-call(f32[128,512]{1,0:T(8,128)S(1)} %get-tuple-element.26.z_ref, f32[128,128]{1,0:T(8,128)S(1)} %get-tuple-element.27.inv_ref, f32[128,128]{1,0:T(8,128)S(1)} %get-tuple-element.28.proj_ref), custom_call_target="tpu_custom_call" | custom-call | tf_op jit(solution)/shard_map/carry/pallas_call | solution.py:314
  81.1 1.0 collective-permute-done.18.b_ref
  82.1 5.9 %pair_node.1 = (f32[128,128]{1,0:T(8,128)S(1)}, f32[128,128]{1,0:T(8,128)S(1)}, f32[128,128]{1,0:T(8,128)S(1)}) custom-call(f32[128,128]{1,0:T(8,128)S(1)} %get-tuple-element.30.a_ref, f32[128,128]{1,0:T(8,128)S(1)} %collective-permute-done.18.b_ref), custom_call_target="tpu_custom_call" | custom-call | tf_op jit(solution)/shard_map/pair_node/pallas_call | solution.py:310
  87.9 1.7 %collective-permute-start.19 = (f32[128,128]{1,0:T(8,128)S(1)}, f32[128,128]{1,0:T(8,128)S(1)}, u32[]{:S(2)}, u32[]{:S(2)}) collective-permute-start(f32[128,128]{1,0:T(8,128)S(1)} %get-tuple-element.33.a_ref), channel_id=1, source_target_pairs={{0,2},{1,3},{2,0},{3,1},{4,6},{5,7},{6,4},{7,5},{8,10},{9,11},{10,... | collective-permute-start | bytes 196616 | tf_op jit(solution)/shard_map/ppermute | solution.py:335
  89.7 1.0 carry2.1.z_ref
  90.7 3.4 %collective-permute-done.19.b_ref = f32[128,128]{1,0:T(8,128)S(1)} collective-permute-done((f32[128,128]{1,0:T(8,128)S(1)}, f32[128,128]{1,0:T(8,128)S(1)}, u32[]{:S(2)}, u32[]{:S(2)}) %collective-permute-start.19) | collective-permute-done | bytes 65568 | tf_op jit(solution)/shard_map/ppermute | solution.py:335
  94.1 6.6 %last_node.1 = f32[512,128]{1,0:T(8,128)} custom-call(f32[128,128]{1,0:T(8,128)S(1)} %get-tuple-element.33.a_ref, f32[128,128]{1,0:T(8,128)S(1)} %collective-permute-done.19.b_ref, f32[512,128]{1,0:T(8,128)S(1)} %carry2.1.z_ref), custom_call_target="tpu_custom_call" | custom-call | tf_op jit(solution)/shard_map/last_node/pallas_call | solution.py:322
  (33 shorter events, 4.2 us)
Async XLA Ops:
  1.4 3.6 %collective-permute-start = (bf16[8,1024]{1,0:T(8,128)(2,1)S(1)}, bf16[8,1024]{1,0:T(8,128)(2,1)S(1)}, u32[]{:S(2)}, u32[]{:S(2)}) collective-permute-start(bf16[8,1024]{1,0:T(8,128)(2,1)S(1)} %get-tuple-element.41), channel_id=1, source_target_pairs={{0,16},{16,0},{1,17},{17,1},{2,18},{18,2},{3,19},{19,3},{4,20},{20... | collective-permute-start | bytes 49160 | tf_op jit(solution)/shard_map/ppermute | solution.py:335
  1.4 5.8 %collective-permute-start.2 = (bf16[8,1024]{1,0:T(8,128)(2,1)S(1)}, bf16[8,1024]{1,0:T(8,128)(2,1)S(1)}, u32[]{:S(2)}, u32[]{:S(2)}) collective-permute-start(bf16[8,1024]{1,0:T(8,128)(2,1)S(1)} %get-tuple-element.41), channel_id=1, source_target_pairs={{0,48},{16,32},{32,16},{48,0},{64,112},{80,96},{96,80},{112,64},{1... | collective-permute-start | bytes 49160 | tf_op jit(solution)/shard_map/ppermute | solution.py:339
  3.4 3.7 %collective-permute-start.1 = (bf16[8,1024]{1,0:T(8,128)(2,1)S(1)}, bf16[8,1024]{1,0:T(8,128)(2,1)S(1)}, u32[]{:S(2)}, u32[]{:S(2)}) collective-permute-start(bf16[8,1024]{1,0:T(8,128)(2,1)S(1)} %get-tuple-element.40), channel_id=1, source_target_pairs={{0,32},{32,0},{64,96},{96,64},{128,160},{160,128},{192,224},{224,1... | collective-permute-start | bytes 49160 | tf_op jit(solution)/shard_map/ppermute | solution.py:335
  3.5 14.2 %collective-permute-start.6 = (f32[3,2048]{1,0:T(4,128)}, f32[3,2048]{1,0:T(4,128)S(1)}, u32[]{:S(2)}, u32[]{:S(2)}) collective-permute-start(f32[3,2048]{1,0:T(4,128)} %src_ref.1), channel_id=1, source_target_pairs={{0,4},{4,0},{8,12},{12,8},{1,5},{5,1},{9,13},{13,9},{2,6},{6,2},{1... | collective-permute-start | bytes 73736 | tf_op jit(solution)/shard_map/ppermute | solution.py:335
  7.2 22.2 %collective-permute-start.3 = (bf16[32,1024]{1,0:T(8,128)(2,1)S(1)}, bf16[32,1024]{1,0:T(8,128)(2,1)S(1)}, u32[]{:S(2)}, u32[]{:S(2)}) collective-permute-start(bf16[32,1024]{1,0:T(8,128)(2,1)S(1)} %get-tuple-element.39), channel_id=1, source_target_pairs={{0,64},{32,96},{64,128},{96,160},{128,192},{160,224},{192,0},{224,... | collective-permute-start | bytes 196616 | tf_op jit(solution)/shard_map/ppermute | solution.py:331
  10.5 18.9 %collective-permute-start.4 = (bf16[32,1024]{1,0:T(8,128)(2,1)S(1)}, bf16[32,1024]{1,0:T(8,128)(2,1)S(1)}, u32[]{:S(2)}, u32[]{:S(2)}) collective-permute-start(bf16[32,1024]{1,0:T(8,128)(2,1)S(1)} %get-tuple-element.39), channel_id=1, source_target_pairs={{0,128},{32,160},{64,192},{96,224},{128,0},{160,32},{192,64},{224,... | collective-permute-start | bytes 196616 | tf_op jit(solution)/shard_map/ppermute | solution.py:331
  15.0 14.4 %collective-permute-start.5 = (bf16[32,1024]{1,0:T(8,128)(2,1)S(1)}, bf16[32,1024]{1,0:T(8,128)(2,1)S(1)}, u32[]{:S(2)}, u32[]{:S(2)}) collective-permute-start(bf16[32,1024]{1,0:T(8,128)(2,1)S(1)} %get-tuple-element.39), channel_id=1, source_target_pairs={{0,192},{32,224},{64,0},{96,32},{128,64},{160,96},{192,128},{224,1... | collective-permute-start | bytes 196616 | tf_op jit(solution)/shard_map/ppermute | solution.py:331
  18.5 11.1 %collective-permute-start.8 = (f32[2,3,2048]{2,1,0:T(4,128)S(1)}, f32[2,3,2048]{2,1,0:T(4,128)S(1)}, u32[]{:S(2)}, u32[]{:S(2)}) collective-permute-start(f32[2,3,2048]{2,1,0:T(4,128)S(1)} %pad_maximum_fusion.2), channel_id=1, source_target_pairs={{0,8},{4,12},{8,0},{12,4},{1,9},{5,13},{9,1},{13,5},{2,10},{6,14},... | collective-permute-start | bytes 147464 | tf_op jit(solution)/shard_map/ppermute | solution.py:335
  21.6 0.9 copy-start
  22.5 0.7 copy-start.1
  29.5 4.3 %collective-permute-start.7 = (bf16[4,32,1024]{2,1,0:T(8,128)(2,1)S(1)}, bf16[4,32,1024]{2,1,0:T(8,128)(2,1)S(1)}, u32[]{:S(2)}, u32[]{:S(2)}) collective-permute-start(bf16[4,32,1024]{2,1,0:T(8,128)(2,1)S(1)} %pad_maximum_fusion.mine_ref), channel_id=1, source_target_pairs={{0,16},{16,0},{1,17},{17,1},{2,18},{18,2},{3,19},{19,3},{4,20},{20... | collective-permute-start | bytes 786440 | tf_op jit(solution)/shard_map/ppermute | solution.py:335
  29.6 16.8 %collective-permute-start.11 = (bf16[4,32,1024]{2,1,0:T(8,128)(2,1)S(1)}, bf16[4,32,1024]{2,1,0:T(8,128)(2,1)S(1)}, u32[]{:S(2)}, u32[]{:S(2)}) collective-permute-start(bf16[4,32,1024]{2,1,0:T(8,128)(2,1)S(1)} %pad_maximum_fusion.mine_ref), channel_id=1, source_target_pairs={{0,12},{4,8},{8,4},{12,0},{1,13},{5,9},{9,5},{13,1},{2,14},{6,10},... | collective-permute-start | bytes 786440 | tf_op jit(solution)/shard_map/ppermute | solution.py:335
  30.9 15.9 %collective-permute-start.10 = (bf16[4,32,1024]{2,1,0:T(8,128)(2,1)S(1)}, bf16[4,32,1024]{2,1,0:T(8,128)(2,1)S(1)}, u32[]{:S(2)}, u32[]{:S(2)}) collective-permute-start(bf16[4,32,1024]{2,1,0:T(8,128)(2,1)S(1)} %pad_maximum_fusion.mine_ref), channel_id=1, source_target_pairs={{0,8},{4,12},{8,0},{12,4},{1,9},{5,13},{9,1},{13,5},{2,10},{6,14},... | collective-permute-start | bytes 786440 | tf_op jit(solution)/shard_map/ppermute | solution.py:335
  32.4 14.9 %collective-permute-start.9 = (bf16[4,32,1024]{2,1,0:T(8,128)(2,1)S(1)}, bf16[4,32,1024]{2,1,0:T(8,128)(2,1)S(1)}, u32[]{:S(2)}, u32[]{:S(2)}) collective-permute-start(bf16[4,32,1024]{2,1,0:T(8,128)(2,1)S(1)} %pad_maximum_fusion.mine_ref), channel_id=1, source_target_pairs={{0,4},{4,0},{8,12},{12,8},{1,5},{5,1},{9,13},{13,9},{2,6},{6,2},{1... | collective-permute-start | bytes 786440 | tf_op jit(solution)/shard_map/ppermute | solution.py:335
  33.8 4.8 %copy-start.2 = (f32[3,2048]{1,0:T(4,128)S(1)}, f32[3,2048]{1,0:T(4,128)}, u32[]{:S(2)}) copy-start(f32[3,2048]{1,0:T(4,128)} %src_ref.1) | copy-start | bytes 73732
  46.4 1.8 %collective-permute-start.14 = (bf16[4,32,1024]{2,1,0:T(8,128)(2,1)S(1)}, bf16[4,32,1024]{2,1,0:T(8,128)(2,1)S(1)}, u32[]{:S(2)}, u32[]{:S(2)}) collective-permute-start(bf16[4,32,1024]{2,1,0:T(8,128)(2,1)S(1)} %collective-permute-done.11.refs_5_.refs_4_), channel_id=1, source_target_pairs={{0,16},{16,0},{1,17},{17,1},{2,18},{18,2},{3,19},{19,3},{4,20},{20... | collective-permute-start | bytes 786440 | tf_op jit(solution)/shard_map/ppermute | solution.py:335
  46.7 1.9 %collective-permute-start.13 = (bf16[4,32,1024]{2,1,0:T(8,128)(2,1)S(1)}, bf16[4,32,1024]{2,1,0:T(8,128)(2,1)S(1)}, u32[]{:S(2)}, u32[]{:S(2)}) collective-permute-start(bf16[4,32,1024]{2,1,0:T(8,128)(2,1)S(1)} %collective-permute-done.10.refs_4_.refs_5_), channel_id=1, source_target_pairs={{0,16},{16,0},{1,17},{17,1},{2,18},{18,2},{3,19},{19,3},{4,20},{20... | collective-permute-start | bytes 786440 | tf_op jit(solution)/shard_map/ppermute | solution.py:335
  47.2 1.8 %collective-permute-start.12 = (bf16[4,32,1024]{2,1,0:T(8,128)(2,1)S(1)}, bf16[4,32,1024]{2,1,0:T(8,128)(2,1)S(1)}, u32[]{:S(2)}, u32[]{:S(2)}) collective-permute-start(bf16[4,32,1024]{2,1,0:T(8,128)(2,1)S(1)} %collective-permute-done.9.refs_3_), channel_id=1, source_target_pairs={{0,16},{16,0},{1,17},{17,1},{2,18},{18,2},{3,19},{19,3},{4,20},{20... | collective-permute-start | bytes 786440 | tf_op jit(solution)/shard_map/ppermute | solution.py:335
  51.7 14.7 %collective-permute-start.17 = (f32[128,512]{1,0:T(8,128)S(1)}, f32[128,512]{1,0:T(8,128)S(1)}, u32[]{:S(2)}, u32[]{:S(2)}) collective-permute-start(f32[128,512]{1,0:T(8,128)S(1)} %leaf_sums.7), channel_id=1, source_target_pairs={{0,3},{1,0},{2,1},{3,2},{4,7},{5,4},{6,5},{7,6},{8,11},{9,8},{10,9... | collective-permute-start | bytes 786440 | tf_op jit(solution)/shard_map/ppermute | solution.py:331
  55.0 11.8 %collective-permute-start.16 = (f32[128,512]{1,0:T(8,128)S(1)}, f32[128,512]{1,0:T(8,128)S(1)}, u32[]{:S(2)}, u32[]{:S(2)}) collective-permute-start(f32[128,512]{1,0:T(8,128)S(1)} %leaf_sums.6), channel_id=1, source_target_pairs={{0,2},{1,3},{2,0},{3,1},{4,6},{5,7},{6,4},{7,5},{8,10},{9,11},{10,... | collective-permute-start | bytes 786440 | tf_op jit(solution)/shard_map/ppermute | solution.py:331
  60.4 10.0 %collective-permute-start.15 = (f32[128,512]{1,0:T(8,128)S(1)}, f32[128,512]{1,0:T(8,128)S(1)}, u32[]{:S(2)}, u32[]{:S(2)}) collective-permute-start(f32[128,512]{1,0:T(8,128)S(1)} %leaf_sums.5), channel_id=1, source_target_pairs={{0,1},{1,2},{2,3},{3,0},{4,5},{5,6},{6,7},{7,4},{8,9},{9,10},{10,1... | collective-permute-start | bytes 786440 | tf_op jit(solution)/shard_map/ppermute | solution.py:331
  76.8 5.3 %collective-permute-start.18 = (f32[128,128]{1,0:T(8,128)S(1)}, f32[128,128]{1,0:T(8,128)S(1)}, u32[]{:S(2)}, u32[]{:S(2)}) collective-permute-start(f32[128,128]{1,0:T(8,128)S(1)} %get-tuple-element.30.a_ref), channel_id=1, source_target_pairs={{0,1},{1,0},{2,3},{3,2},{4,5},{5,4},{6,7},{7,6},{8,9},{9,8},{10,11... | collective-permute-start | bytes 196616 | tf_op jit(solution)/shard_map/ppermute | solution.py:335
  87.9 6.1 %collective-permute-start.19 = (f32[128,128]{1,0:T(8,128)S(1)}, f32[128,128]{1,0:T(8,128)S(1)}, u32[]{:S(2)}, u32[]{:S(2)}) collective-permute-start(f32[128,128]{1,0:T(8,128)S(1)} %get-tuple-element.33.a_ref), channel_id=1, source_target_pairs={{0,2},{1,3},{2,0},{3,1},{4,6},{5,7},{6,4},{7,5},{8,10},{9,11},{10,... | collective-permute-start | bytes 196616 | tf_op jit(solution)/shard_map/ppermute | solution.py:335
where the time goes:
time: 102 us; the launch traced here: 101 us
  Pallas kernels  52.1 us (51%)
  starting transfers between devices  32.5 us (32%)
  waiting for transfers between devices  12 us (12%)
  local copies, waits for them, and re-layouts  2.35 us (2%)
    ppermute x6, starting transfers between devices, moved(): return lax.ppermute(x, axis, [(i, (i + by) % size) for i in range(size)])  15.9 us
    ppermute x13, starting transfers between devices, crossed(): lax.ppermute(x, axis, [(i, i ^ bit) for i in range(lax.axis_size(axis))])  14.6 us
    pallas_call x4, Pallas kernels, leaf_sums(): pl.pallas_call(functools.partial(sums_body, turn, stored, fused), out_sha...  12.1 us
    pallas_call x2, Pallas kernels, kernel_tiles(): pl.pallas_call(functools.partial(tiles_body, q, first), out_shape=jax.Sha...  11.1 us
    ppermute x13, waiting for transfers between devices, crossed(): lax.ppermute(x, axis, [(i, i ^ bit) for i in range(lax.axis_size(axis))])  8.14 us
    pallas_call x1, Pallas kernels, own_sums(): pl.pallas_call(own_body, out_shape=jax.ShapeDtypeStruct((4, 128, LEAF), F...  7.75 us
    pallas_call x1, Pallas kernels, last_node(): pl.pallas_call(last_body, out_shape=sds(512, 128), scratch_shapes=SCR, na...  6.65 us
    pallas_call x1, Pallas kernels, leaf_node(): pl.pallas_call(leaf_body, out_shape=(sds(128, LEAF),) + (sds(128, 128),)...  6.42 us
  transfers between devices with their start and end apart: 20, of which 8 were waited for; matrix products, arithmetic and copies ran while one was open for 1% of the time, Pallas kernels for 30%

commit v1 on v0

--- a/solution.py
+++ b/solution.py
@@ -180,6 +180,21 @@
       *[mine[q] for q in order], *[other[q] for q in order])
 
 
+def spread(x, lane):
+    return jnp.take_along_axis(x, jnp.full(x.shape, lane, jnp.int32), axis=1, mode="promise_in_bounds")
+
+
+def row(x, k):
+    return jnp.broadcast_to(x[k:k + 1, :], x.shape)
+
+
+def pivots(cols, k):
+    a, off, d = row(cols[k], k), row(cols[k], k + 1), row(cols[k + 1], k + 1)
+    inv = lax.rsqrt(a)
+    rest = lax.rsqrt(a * d - off * off)
+    return (inv, (a * inv) * rest), (inv * inv, a * (rest * rest))
+
+
 def eliminate(gram, aug_ref, top_ref):
     n = 128
     i = lax.broadcasted_iota(jnp.int32, (n, n), 0)
@@ -188,39 +203,54 @@
     aug_ref[:, n:] = jnp.where(i == j, 1.0, 0.0)
     sub = lax.broadcasted_iota(jnp.int32, (8, n), 0)
     lane = lax.broadcasted_iota(jnp.int32, (8, n), 1)
-    for b in range(n // 8):
-        at = 8 * b
-        left = aug_ref[at:at + 8, :n]
-        right = aug_ref[at:at + 8, n:]
-        cols = [jnp.broadcast_to(left[:, at + k:at + k + 1], (8, n)) for k in range(8)]
-        scale = jnp.zeros((8, n), F32)
+    for at in range(0, n, 16):
+        high = [aug_ref[at:at + 8, :n], aug_ref[at:at + 8, n:]]
+        low = [aug_ref[at + 8:at + 16, :n], aug_ref[at + 8:at + 16, n:]]
+        upper = [spread(high[0], at + k) for k in range(8)]
+        under = [spread(low[0], at + k) for k in range(8)]
+        lower = [spread(low[0], at + 8 + k) for k in range(8)]
+        scale_high = scale_low = jnp.zeros((8, n), F32)
         for k in range(0, 8, 2):
-            a = jnp.broadcast_to(cols[k][k:k + 1, :], (8, n))
-            off = jnp.broadcast_to(cols[k + 1][k:k + 1, :], (8, n))
-            d = jnp.broadcast_to(cols[k + 1][k + 1:k + 2, :], (8, n))
-            inv = lax.rsqrt(a)
-            rest = lax.rsqrt(a * d - off * off)
-            scale = jnp.where(sub == k, inv, jnp.where(sub == k + 1, (a * inv) * rest, scale))
-            for j, square in ((k, inv * inv), (k + 1, a * (rest * rest))):
-                if j < 7:
-                    mult = jnp.where(sub > j, cols[j] * square, 0.0)
-                    for q in range(j + 1, 8):
-                        cols[q] = cols[q] - mult * jnp.broadcast_to(cols[q][j:j + 1, :], (8, n))
-                    left = left - mult * jnp.broadcast_to(left[j:j + 1, :], (8, n))
-                    right = right - mult * jnp.broadcast_to(right[j:j + 1, :], (8, n))
-        left = jnp.where(lane >= sub + at, left * scale, 0.0)
-        right = right * scale
-        top_ref[at:at + 8, :n] = left
-        top_ref[at:at + 8, n:] = right
-        if b < n // 8 - 1:
-            l1, l2, l3 = parts3(left)
-            r1, r2, r3 = parts3(right)
+            scales, squares = pivots(upper, k)
+            scale_high = jnp.where(sub == k, scales[0], jnp.where(sub == k + 1, scales[1], scale_high))
+            for p, square in ((k, squares[0]), (k + 1, squares[1])):
+                mult = jnp.where(sub > p, upper[p] * square, 0.0)
+                wide = under[p] * square
+                for q in range(p + 1, 8):
+                    entry = row(upper[p], q)
+                    upper[q] = upper[q] - mult * entry
+                    under[q] = under[q] - wide * entry
+                for q in range(8):
+                    lower[q] = lower[q] - wide * row(under[p], q)
+                for h in range(2):
+                    line = row(high[h], p)
+                    low[h] = low[h] - wide * line
+                    if p < 7:
+                        high[h] = high[h] - mult * line
+        for k in range(0, 8, 2):
+            scales, squares = pivots(lower, k)
+            scale_low = jnp.where(sub == k, scales[0], jnp.where(sub == k + 1, scales[1], scale_low))
+            for p, square in ((k, squares[0]), (k + 1, squares[1])):
+                if p < 7:
+                    mult = jnp.where(sub > p, lower[p] * square, 0.0)
+                    for q in range(p + 1, 8):
+                        lower[q] = lower[q] - mult * row(lower[p], q)
+                    for h in range(2):
+                        low[h] = low[h] - mult * row(low[h], p)
+        left = [jnp.where(lane >= sub + at, high[0] * scale_high, 0.0), jnp.where(lane >= sub + at + 8, low[0] * scale_low, 0.0)]
+        right = [high[1] * scale_high, low[1] * scale_low]
+        for h in range(2):
+            top_ref[at + 8 * h:at + 8 * h + 8, :n] = left[h]
+            top_ref[at + 8 * h:at + 8 * h + 8, n:] = right[h]
+        if at < n - 16:
+            l1, l2, l3 = parts3(jnp.concatenate(left, axis=0))
+            r1, r2, r3 = parts3(jnp.concatenate(right, axis=0))
             lhs = jnp.concatenate([l1, l1, l2, l1, l2, l3], axis=0).astype(BF)
             rl = jnp.concatenate([l1, l2, l1, l3, l2, l1], axis=0)
             rr = jnp.concatenate([r1, r2, r1, r3, r2, r1], axis=0)
             rhs = jnp.concatenate([rl, rr], axis=1).astype(BF)
             upd = lax.dot_general(lhs, rhs, (((0,), (0,)), ((), ())), preferred_element_type=F32)
-            aug_ref[at + 8:, :] -= upd[at + 8:, :]
+            aug_ref[at + 16:, :] -= upd[at + 16:, :]
 
 
 def regular(gram):

time: 102 us -> 93.7 us (0.919)
  Pallas kernels: 52.1 us -> 44.4 us
    pallas_call x1, Pallas kernels: 6.42 us -> 3.84 us  [leaf_node(): pl.pallas_call(leaf_body, out_shape=(sds(128, LEAF),) + (sds(128, 128),)...]
    pallas_call x1, Pallas kernels: 5.88 us -> 3.3 us  [pair_node(): pl.pallas_call(node_body, out_shape=(sds(128, 128),) * 3, scratch_shapes=...]
    pallas_call x1, Pallas kernels: 6.65 us -> 4.08 us  [last_node(): pl.pallas_call(last_body, out_shape=sds(512, 128), scratch_shapes=SCR, na...]
  transfers between devices with their start and end apart: 20 -> 20, of which waited for: 8 -> 8; matrix products, arithmetic and copies ran while one was open for 1% -> 1% of each run, Pallas kernels for 30% -> 33%
where the time goes in v1:
time: 93.7 us; the launch traced here: 92.7 us
  Pallas kernels  44.4 us (47%)
  starting transfers between devices  32.2 us (34%)
  waiting for transfers between devices  12.1 us (13%)
  local copies, waits for them, and re-layouts  2.35 us (3%)
    ppermute x6, starting transfers between devices, moved(): return lax.ppermute(x, axis, [(i, (i + by) % size) for i in range(size)])  15.9 us
    ppermute x13, starting transfers between devices, crossed(): lax.ppermute(x, axis, [(i, i ^ bit) for i in range(lax.axis_size(axis))])  14.3 us
    pallas_call x4, Pallas kernels, leaf_sums(): pl.pallas_call(functools.partial(sums_body, turn, stored, fused), out_sha...  12.1 us
    pallas_call x2, Pallas kernels, kernel_tiles(): pl.pallas_call(functools.partial(tiles_body, q, first), out_shape=jax.Sha...  11.1 us
    ppermute x13, waiting for transfers between devices, crossed(): lax.ppermute(x, axis, [(i, i ^ bit) for i in range(lax.axis_size(axis))])  8.15 us
    pallas_call x1, Pallas kernels, own_sums(): pl.pallas_call(own_body, out_shape=jax.ShapeDtypeStruct((4, 128, LEAF), F...  7.75 us
    pallas_call x1, Pallas kernels, last_node(): pl.pallas_call(last_body, out_shape=sds(512, 128), scratch_shapes=SCR, na...  4.08 us
    ppermute x6, waiting for transfers between devices, moved(): return lax.ppermute(x, axis, [(i, (i + by) % size) for i in range(size)])  3.9 us
  transfers between devices with their start and end apart: 20, of which 8 were waited for; matrix products, arithmetic and copies ran while one was open for 1% of the time, Pallas kernels for 33%

profile of v1, /device:TPU:8, one launch (start us, length us, event | category | flops | bytes accessed | tf_op | source)
XLA Modules:
  0.0 92.7 jit_solution(5629007762445850300)
XLA Ops:
  1.4 2.0 %collective-permute-start.2 = (bf16[8,1024]{1,0:T(8,128)(2,1)S(1)}, bf16[8,1024]{1,0:T(8,128)(2,1)S(1)}, u32[]{:S(2)}, u32[]{:S(2)}) collective-permute-start(bf16[8,1024]{1,0:T(8,128)(2,1)S(1)} %get-tuple-element.41), channel_id=1, source_target_pairs={{0,48},{16,32},{32,16},{48,0},{64,112},{80,96},{96,80},{112,64},{1... | collective-permute-start | bytes 49160 | tf_op jit(solution)/shard_map/ppermute | solution.py:369
  3.5 1.5 %collective-permute-start.6 = (f32[3,2048]{1,0:T(4,128)}, f32[3,2048]{1,0:T(4,128)S(1)}, u32[]{:S(2)}, u32[]{:S(2)}) collective-permute-start(f32[3,2048]{1,0:T(4,128)} %src_ref.1), channel_id=1, source_target_pairs={{0,4},{4,0},{8,12},{12,8},{1,5},{5,1},{9,13},{13,9},{2,6},{6,2},{1... | collective-permute-start | bytes 73736 | tf_op jit(solution)/shard_map/ppermute | solution.py:365
  5.0 2.1 %collective-permute-done.1 = bf16[8,1024]{1,0:T(8,128)(2,1)S(1)} collective-permute-done((bf16[8,1024]{1,0:T(8,128)(2,1)S(1)}, bf16[8,1024]{1,0:T(8,128)(2,1)S(1)}, u32[]{:S(2)}, u32[]{:S(2)}) %collective-permute-start.1) | collective-permute-done | bytes 16416 | tf_op jit(solution)/shard_map/ppermute | solution.py:365
  7.2 3.3 %collective-permute-start.3 = (bf16[32,1024]{1,0:T(8,128)(2,1)S(1)}, bf16[32,1024]{1,0:T(8,128)(2,1)S(1)}, u32[]{:S(2)}, u32[]{:S(2)}) collective-permute-start(bf16[32,1024]{1,0:T(8,128)(2,1)S(1)} %get-tuple-element.39), channel_id=1, source_target_pairs={{0,64},{32,96},{64,128},{96,160},{128,192},{160,224},{192,0},{224,... | collective-permute-start | bytes 196616 | tf_op jit(solution)/shard_map/ppermute | solution.py:361
  10.5 4.5 %collective-permute-start.4 = (bf16[32,1024]{1,0:T(8,128)(2,1)S(1)}, bf16[32,1024]{1,0:T(8,128)(2,1)S(1)}, u32[]{:S(2)}, u32[]{:S(2)}) collective-permute-start(bf16[32,1024]{1,0:T(8,128)(2,1)S(1)} %get-tuple-element.39), channel_id=1, source_target_pairs={{0,128},{32,160},{64,192},{96,224},{128,0},{160,32},{192,64},{224,... | collective-permute-start | bytes 196616 | tf_op jit(solution)/shard_map/ppermute | solution.py:361
  15.0 2.7 %collective-permute-start.5 = (bf16[32,1024]{1,0:T(8,128)(2,1)S(1)}, bf16[32,1024]{1,0:T(8,128)(2,1)S(1)}, u32[]{:S(2)}, u32[]{:S(2)}) collective-permute-start(bf16[32,1024]{1,0:T(8,128)(2,1)S(1)} %get-tuple-element.39), channel_id=1, source_target_pairs={{0,192},{32,224},{64,0},{96,32},{128,64},{160,96},{192,128},{224,1... | collective-permute-start | bytes 196616 | tf_op jit(solution)/shard_map/ppermute | solution.py:361
  17.7 0.8 pad_maximum_fusion.2
  18.5 3.1 %collective-permute-start.8 = (f32[2,3,2048]{2,1,0:T(4,128)S(1)}, f32[2,3,2048]{2,1,0:T(4,128)S(1)}, u32[]{:S(2)}, u32[]{:S(2)}) collective-permute-start(f32[2,3,2048]{2,1,0:T(4,128)S(1)} %pad_maximum_fusion.2), channel_id=1, source_target_pairs={{0,8},{4,12},{8,0},{12,4},{1,9},{5,13},{9,1},{13,5},{2,10},{6,14},... | collective-permute-start | bytes 147464 | tf_op jit(solution)/shard_map/ppermute | solution.py:365
  21.6 0.9 copy-done
  23.2 6.2 %kernel_tiles.2.refs_0_ = bf16[4,2048,512]{2,1,0:T(8,128)(2,1)S(1)} custom-call(s32[8,16]{1,0:T(8,128)S(1)} %bitcast.16, f32[3,8192]{1,0:T(4,128)S(1)} %copy-done, f32[3,2048]{1,0:T(4,128)S(1)} %collective-permute-done.6.src_ref), custom_call_target="tpu_custom_call" | custom-call | flops 8000000000 | bytes 8400000 | tf_op jit(solution)/shard_map/kernel_tiles/pallas_call | solution.py:91
  29.6 1.2 %collective-permute-start.11 = (bf16[4,32,1024]{2,1,0:T(8,128)(2,1)S(1)}, bf16[4,32,1024]{2,1,0:T(8,128)(2,1)S(1)}, u32[]{:S(2)}, u32[]{:S(2)}) collective-permute-start(bf16[4,32,1024]{2,1,0:T(8,128)(2,1)S(1)} %pad_maximum_fusion.mine_ref), channel_id=1, source_target_pairs={{0,12},{4,8},{8,4},{12,0},{1,13},{5,9},{9,5},{13,1},{2,14},{6,10},... | collective-permute-start | bytes 786440 | tf_op jit(solution)/shard_map/ppermute | solution.py:365
  30.9 1.5 %collective-permute-start.10 = (bf16[4,32,1024]{2,1,0:T(8,128)(2,1)S(1)}, bf16[4,32,1024]{2,1,0:T(8,128)(2,1)S(1)}, u32[]{:S(2)}, u32[]{:S(2)}) collective-permute-start(bf16[4,32,1024]{2,1,0:T(8,128)(2,1)S(1)} %pad_maximum_fusion.mine_ref), channel_id=1, source_target_pairs={{0,8},{4,12},{8,0},{12,4},{1,9},{5,13},{9,1},{13,5},{2,10},{6,14},... | collective-permute-start | bytes 786440 | tf_op jit(solution)/shard_map/ppermute | solution.py:365
  32.4 1.4 %collective-permute-start.9 = (bf16[4,32,1024]{2,1,0:T(8,128)(2,1)S(1)}, bf16[4,32,1024]{2,1,0:T(8,128)(2,1)S(1)}, u32[]{:S(2)}, u32[]{:S(2)}) collective-permute-start(bf16[4,32,1024]{2,1,0:T(8,128)(2,1)S(1)} %pad_maximum_fusion.mine_ref), channel_id=1, source_target_pairs={{0,4},{4,0},{8,12},{12,8},{1,5},{5,1},{9,13},{13,9},{2,6},{6,2},{1... | collective-permute-start | bytes 786440 | tf_op jit(solution)/shard_map/ppermute | solution.py:365
  33.8 4.8 %kernel_tiles.3.refs_1_ = bf16[3,2048,512]{2,1,0:T(8,128)(2,1)S(1)} custom-call(s32[8,16]{1,0:T(8,128)S(1)} %bitcast.17, f32[3,8192]{1,0:T(4,128)S(1)} %copy-done, f32[3,2048]{1,0:T(4,128)S(1)} %get-tuple-element.21.src_ref.refs_2_), custom_call_target="tpu_custom_call" | custom-call | flops 8000000000 | bytes 8400000 | tf_op jit(solution)/shard_map/kernel_tiles/pallas_call | solution.py:91
  38.7 7.8 %own_sums.1.base_ref = f32[4,128,512]{2,1,0:T(8,128)S(1)} custom-call(s32[8,16]{1,0:T(8,128)S(1)} %bitcast.18, f32[3,8192]{1,0:T(4,128)S(1)} %copy-done, f32[3,2048]{1,0:T(4,128)S(1)} %copy-done.2, bf16[4,32,1024]{2,1,0:T(8,128)(2,1)S(1)} %pad_maximum_fusion.mine_ref, bf16[4,32,1024]{2,1,0:T(8,128)(2,1)S(1)} %collective-permute-done.7.other_ref), custom_call_target="tpu_custom_call" | custom-call | flops 8000000000 | bytes 8400000 | tf_op jit(solution)/shard_map/own_sums/pallas_call | solution.py:125
  47.3 0.9 collective-permute-done.14.refs_8_.refs_7_
  49.0 2.7 %leaf_sums.7 = f32[128,512]{1,0:T(8,128)S(1)} custom-call(s32[8,16]{1,0:T(8,128)S(1)} %bitcast.19, f32[3,8192]{1,0:T(4,128)S(1)} %copy-done, f32[4,128,512]{2,1,0:T(8,128)S(1)} %own_sums.1.base_ref, bf16[4,2048,512]{2,1,0:T(8,128)(2,1)S(1)} %kernel_tiles.2.refs_0_, bf16[3,2048,512]{2,1,0:T(8,128)(2,1)S(1)} %kernel_tiles.3.refs_1_, ...), custom_call_target="tpu_custom_call" | custom-call | flops 4000000000 | bytes 9000000 | tf_op jit(solution)/shard_map/leaf_sums/pallas_call | solution.py:167
  52.3 2.7 %leaf_sums.6 = f32[128,512]{1,0:T(8,128)S(1)} custom-call(s32[8,16]{1,0:T(8,128)S(1)} %bitcast.20, f32[3,8192]{1,0:T(4,128)S(1)} %copy-done, f32[4,128,512]{2,1,0:T(8,128)S(1)} %own_sums.1.base_ref, bf16[4,2048,512]{2,1,0:T(8,128)(2,1)S(1)} %kernel_tiles.2.refs_0_, bf16[3,2048,512]{2,1,0:T(8,128)(2,1)S(1)} %kernel_tiles.3.refs_1_, ...), custom_call_target="tpu_custom_call" | custom-call | flops 4000000000 | bytes 9000000 | tf_op jit(solution)/shard_map/leaf_sums/pallas_call | solution.py:167
  55.0 2.7 %collective-permute-start.16 = (f32[128,512]{1,0:T(8,128)S(1)}, f32[128,512]{1,0:T(8,128)S(1)}, u32[]{:S(2)}, u32[]{:S(2)}) collective-permute-start(f32[128,512]{1,0:T(8,128)S(1)} %leaf_sums.6), channel_id=1, source_target_pairs={{0,2},{1,3},{2,0},{3,1},{4,6},{5,7},{6,4},{7,5},{8,10},{9,11},{10,... | collective-permute-start | bytes 786440 | tf_op jit(solution)/shard_map/ppermute | solution.py:361
  57.6 2.7 %leaf_sums.5 = f32[128,512]{1,0:T(8,128)S(1)} custom-call(s32[8,16]{1,0:T(8,128)S(1)} %bitcast.21, f32[3,8192]{1,0:T(4,128)S(1)} %copy-done, f32[4,128,512]{2,1,0:T(8,128)S(1)} %own_sums.1.base_ref, bf16[4,2048,512]{2,1,0:T(8,128)(2,1)S(1)} %kernel_tiles.2.refs_0_, bf16[3,2048,512]{2,1,0:T(8,128)(2,1)S(1)} %kernel_tiles.3.refs_1_, ...), custom_call_target="tpu_custom_call" | custom-call | flops 4000000000 | bytes 9000000 | tf_op jit(solution)/shard_map/leaf_sums/pallas_call | solution.py:167
  60.4 2.2 %collective-permute-start.15 = (f32[128,512]{1,0:T(8,128)S(1)}, f32[128,512]{1,0:T(8,128)S(1)}, u32[]{:S(2)}, u32[]{:S(2)}) collective-permute-start(f32[128,512]{1,0:T(8,128)S(1)} %leaf_sums.5), channel_id=1, source_target_pairs={{0,1},{1,2},{2,3},{3,0},{4,5},{5,6},{6,7},{7,4},{8,9},{9,10},{10,1... | collective-permute-start | bytes 786440 | tf_op jit(solution)/shard_map/ppermute | solution.py:361
  62.6 3.9 %leaf_sums.4.a_ref = f32[128,512]{1,0:T(8,128)S(1)} custom-call(s32[8,16]{1,0:T(8,128)S(1)} %bitcast.22, f32[3,8192]{1,0:T(4,128)S(1)} %copy-done, f32[4,128,512]{2,1,0:T(8,128)S(1)} %own_sums.1.base_ref, bf16[4,2048,512]{2,1,0:T(8,128)(2,1)S(1)} %kernel_tiles.2.refs_0_, f32[3,2048]{1,0:T(4,128)S(1)} %get-tuple-element.36.refs_1_.refs_2_, ...), custom_call_target="tpu_custom_call" | custom-call | flops 4000000000 | bytes 9000000 | tf_op jit(solution)/shard_map/leaf_sums/pallas_call | solution.py:167
  66.8 3.6 %collective-permute-done.15.b_ref = f32[128,512]{1,0:T(8,128)S(1)} collective-permute-done((f32[128,512]{1,0:T(8,128)S(1)}, f32[128,512]{1,0:T(8,128)S(1)}, u32[]{:S(2)}, u32[]{:S(2)}) %collective-permute-start.15) | collective-permute-done | bytes 262176 | tf_op jit(solution)/shard_map/ppermute | solution.py:361
  70.4 3.8 %leaf_node.1 = (f32[128,512]{1,0:T(8,128)S(1)}, f32[128,128]{1,0:T(8,128)S(1)}, f32[128,128]{1,0:T(8,128)S(1)}, f32[128,128]{1,0:T(8,128)S(1)}) custom-call(f32[128,512]{1,0:T(8,128)S(1)} %leaf_sums.4.a_ref, f32[128,512]{1,0:T(8,128)S(1)} %collective-permute-done.15.b_ref, f32[128,512]{1,0:T(8,128)S(1)} %collective-permute-done.16.c_ref, ...), custom_call_target="tpu_custom_call" | custom-call | tf_op jit(solution)/shard_map/leaf_node/pallas_call | solution.py:329
  74.2 3.0 %collective-permute-start.18 = (f32[128,128]{1,0:T(8,128)S(1)}, f32[128,128]{1,0:T(8,128)S(1)}, u32[]{:S(2)}, u32[]{:S(2)}) collective-permute-start(f32[128,128]{1,0:T(8,128)S(1)} %get-tuple-element.30.a_ref), channel_id=1, source_target_pairs={{0,1},{1,0},{2,3},{3,2},{4,5},{5,4},{6,7},{7,6},{8,9},{9,8},{10,11... | collective-permute-start | bytes 196616 | tf_op jit(solution)/shard_map/ppermute | solution.py:365
  77.2 1.3 %carry.1 = (f32[512,128]{1,0:T(8,128)}, f32[512,128]{1,0:T(8,128)S(1)}) custom-call(f32[128,512]{1,0:T(8,128)S(1)} %get-tuple-element.26.z_ref, f32[128,128]{1,0:T(8,128)S(1)} %get-tuple-element.27.inv_ref, f32[128,128]{1,0:T(8,128)S(1)} %get-tuple-element.28.proj_ref), custom_call_target="tpu_custom_call" | custom-call | tf_op jit(solution)/shard_map/carry/pallas_call | solution.py:344
  78.5 1.0 %collective-permute-done.18.b_ref = f32[128,128]{1,0:T(8,128)S(1)} collective-permute-done((f32[128,128]{1,0:T(8,128)S(1)}, f32[128,128]{1,0:T(8,128)S(1)}, u32[]{:S(2)}, u32[]{:S(2)}) %collective-permute-start.18) | collective-permute-done | bytes 65568 | tf_op jit(solution)/shard_map/ppermute | solution.py:365
  79.5 3.3 %pair_node.1 = (f32[128,128]{1,0:T(8,128)S(1)}, f32[128,128]{1,0:T(8,128)S(1)}, f32[128,128]{1,0:T(8,128)S(1)}) custom-call(f32[128,128]{1,0:T(8,128)S(1)} %get-tuple-element.30.a_ref, f32[128,128]{1,0:T(8,128)S(1)} %collective-permute-done.18.b_ref), custom_call_target="tpu_custom_call" | custom-call | tf_op jit(solution)/shard_map/pair_node/pallas_call | solution.py:340
  82.8 1.5 %collective-permute-start.19 = (f32[128,128]{1,0:T(8,128)S(1)}, f32[128,128]{1,0:T(8,128)S(1)}, u32[]{:S(2)}, u32[]{:S(2)}) collective-permute-start(f32[128,128]{1,0:T(8,128)S(1)} %get-tuple-element.33.a_ref), channel_id=1, source_target_pairs={{0,2},{1,3},{2,0},{3,1},{4,6},{5,7},{6,4},{7,5},{8,10},{9,11},{10,... | collective-permute-start | bytes 196616 | tf_op jit(solution)/shard_map/ppermute | solution.py:365
  84.3 1.0 %carry2.1.z_ref = f32[512,128]{1,0:T(8,128)S(1)} custom-call(f32[512,128]{1,0:T(8,128)S(1)} %get-tuple-element.31.z_ref, f32[128,128]{1,0:T(8,128)S(1)} %get-tuple-element.34.inv_ref, f32[128,128]{1,0:T(8,128)S(1)} %get-tuple-element.35.proj_ref), custom_call_target="tpu_custom_call" | custom-call | tf_op jit(solution)/shard_map/carry2/pallas_call | solution.py:348
  85.3 3.4 %collective-permute-done.19.b_ref = f32[128,128]{1,0:T(8,128)S(1)} collective-permute-done((f32[128,128]{1,0:T(8,128)S(1)}, f32[128,128]{1,0:T(8,128)S(1)}, u32[]{:S(2)}, u32[]{:S(2)}) %collective-permute-start.19) | collective-permute-done | bytes 65568 | tf_op jit(solution)/shard_map/ppermute | solution.py:365
  88.6 4.1 %last_node.1 = f32[512,128]{1,0:T(8,128)} custom-call(f32[128,128]{1,0:T(8,128)S(1)} %get-tuple-element.33.a_ref, f32[128,128]{1,0:T(8,128)S(1)} %collective-permute-done.19.b_ref, f32[512,128]{1,0:T(8,128)S(1)} %carry2.1.z_ref), custom_call_target="tpu_custom_call" | custom-call | tf_op jit(solution)/shard_map/last_node/pallas_call | solution.py:352
  (33 shorter events, 4.2 us)
Async XLA Ops:
  1.4 3.6 %collective-permute-start = (bf16[8,1024]{1,0:T(8,128)(2,1)S(1)}, bf16[8,1024]{1,0:T(8,128)(2,1)S(1)}, u32[]{:S(2)}, u32[]{:S(2)}) collective-permute-start(bf16[8,1024]{1,0:T(8,128)(2,1)S(1)} %get-tuple-element.41), channel_id=1, source_target_pairs={{0,16},{16,0},{1,17},{17,1},{2,18},{18,2},{3,19},{19,3},{4,20},{20... | collective-permute-start | bytes 49160 | tf_op jit(solution)/shard_map/ppermute | solution.py:365
  1.4 5.8 %collective-permute-start.2 = (bf16[8,1024]{1,0:T(8,128)(2,1)S(1)}, bf16[8,1024]{1,0:T(8,128)(2,1)S(1)}, u32[]{:S(2)}, u32[]{:S(2)}) collective-permute-start(bf16[8,1024]{1,0:T(8,128)(2,1)S(1)} %get-tuple-element.41), channel_id=1, source_target_pairs={{0,48},{16,32},{32,16},{48,0},{64,112},{80,96},{96,80},{112,64},{1... | collective-permute-start | bytes 49160 | tf_op jit(solution)/shard_map/ppermute | solution.py:369
  3.4 3.7 %collective-permute-start.1 = (bf16[8,1024]{1,0:T(8,128)(2,1)S(1)}, bf16[8,1024]{1,0:T(8,128)(2,1)S(1)}, u32[]{:S(2)}, u32[]{:S(2)}) collective-permute-start(bf16[8,1024]{1,0:T(8,128)(2,1)S(1)} %get-tuple-element.40), channel_id=1, source_target_pairs={{0,32},{32,0},{64,96},{96,64},{128,160},{160,128},{192,224},{224,1... | collective-permute-start | bytes 49160 | tf_op jit(solution)/shard_map/ppermute | solution.py:365
  3.5 14.2 %collective-permute-start.6 = (f32[3,2048]{1,0:T(4,128)}, f32[3,2048]{1,0:T(4,128)S(1)}, u32[]{:S(2)}, u32[]{:S(2)}) collective-permute-start(f32[3,2048]{1,0:T(4,128)} %src_ref.1), channel_id=1, source_target_pairs={{0,4},{4,0},{8,12},{12,8},{1,5},{5,1},{9,13},{13,9},{2,6},{6,2},{1... | collective-permute-start | bytes 73736 | tf_op jit(solution)/shard_map/ppermute | solution.py:365
  7.2 22.2 %collective-permute-start.3 = (bf16[32,1024]{1,0:T(8,128)(2,1)S(1)}, bf16[32,1024]{1,0:T(8,128)(2,1)S(1)}, u32[]{:S(2)}, u32[]{:S(2)}) collective-permute-start(bf16[32,1024]{1,0:T(8,128)(2,1)S(1)} %get-tuple-element.39), channel_id=1, source_target_pairs={{0,64},{32,96},{64,128},{96,160},{128,192},{160,224},{192,0},{224,... | collective-permute-start | bytes 196616 | tf_op jit(solution)/shard_map/ppermute | solution.py:361
  10.5 18.9 %collective-permute-start.4 = (bf16[32,1024]{1,0:T(8,128)(2,1)S(1)}, bf16[32,1024]{1,0:T(8,128)(2,1)S(1)}, u32[]{:S(2)}, u32[]{:S(2)}) collective-permute-start(bf16[32,1024]{1,0:T(8,128)(2,1)S(1)} %get-tuple-element.39), channel_id=1, source_target_pairs={{0,128},{32,160},{64,192},{96,224},{128,0},{160,32},{192,64},{224,... | collective-permute-start | bytes 196616 | tf_op jit(solution)/shard_map/ppermute | solution.py:361
  15.0 14.4 %collective-permute-start.5 = (bf16[32,1024]{1,0:T(8,128)(2,1)S(1)}, bf16[32,1024]{1,0:T(8,128)(2,1)S(1)}, u32[]{:S(2)}, u32[]{:S(2)}) collective-permute-start(bf16[32,1024]{1,0:T(8,128)(2,1)S(1)} %get-tuple-element.39), channel_id=1, source_target_pairs={{0,192},{32,224},{64,0},{96,32},{128,64},{160,96},{192,128},{224,1... | collective-permute-start | bytes 196616 | tf_op jit(solution)/shard_map/ppermute | solution.py:361
  18.5 11.1 %collective-permute-start.8 = (f32[2,3,2048]{2,1,0:T(4,128)S(1)}, f32[2,3,2048]{2,1,0:T(4,128)S(1)}, u32[]{:S(2)}, u32[]{:S(2)}) collective-permute-start(f32[2,3,2048]{2,1,0:T(4,128)S(1)} %pad_maximum_fusion.2), channel_id=1, source_target_pairs={{0,8},{4,12},{8,0},{12,4},{1,9},{5,13},{9,1},{13,5},{2,10},{6,14},... | collective-permute-start | bytes 147464 | tf_op jit(solution)/shard_map/ppermute | solution.py:365
  21.6 0.9 copy-start
  22.5 0.7 copy-start.1
  29.5 4.3 %collective-permute-start.7 = (bf16[4,32,1024]{2,1,0:T(8,128)(2,1)S(1)}, bf16[4,32,1024]{2,1,0:T(8,128)(2,1)S(1)}, u32[]{:S(2)}, u32[]{:S(2)}) collective-permute-start(bf16[4,32,1024]{2,1,0:T(8,128)(2,1)S(1)} %pad_maximum_fusion.mine_ref), channel_id=1, source_target_pairs={{0,16},{16,0},{1,17},{17,1},{2,18},{18,2},{3,19},{19,3},{4,20},{20... | collective-permute-start | bytes 786440 | tf_op jit(solution)/shard_map/ppermute | solution.py:365
  29.6 16.8 %collective-permute-start.11 = (bf16[4,32,1024]{2,1,0:T(8,128)(2,1)S(1)}, bf16[4,32,1024]{2,1,0:T(8,128)(2,1)S(1)}, u32[]{:S(2)}, u32[]{:S(2)}) collective-permute-start(bf16[4,32,1024]{2,1,0:T(8,128)(2,1)S(1)} %pad_maximum_fusion.mine_ref), channel_id=1, source_target_pairs={{0,12},{4,8},{8,4},{12,0},{1,13},{5,9},{9,5},{13,1},{2,14},{6,10},... | collective-permute-start | bytes 786440 | tf_op jit(solution)/shard_map/ppermute | solution.py:365
  30.9 15.9 %collective-permute-start.10 = (bf16[4,32,1024]{2,1,0:T(8,128)(2,1)S(1)}, bf16[4,32,1024]{2,1,0:T(8,128)(2,1)S(1)}, u32[]{:S(2)}, u32[]{:S(2)}) collective-permute-start(bf16[4,32,1024]{2,1,0:T(8,128)(2,1)S(1)} %pad_maximum_fusion.mine_ref), channel_id=1, source_target_pairs={{0,8},{4,12},{8,0},{12,4},{1,9},{5,13},{9,1},{13,5},{2,10},{6,14},... | collective-permute-start | bytes 786440 | tf_op jit(solution)/shard_map/ppermute | solution.py:365
  32.4 14.9 %collective-permute-start.9 = (bf16[4,32,1024]{2,1,0:T(8,128)(2,1)S(1)}, bf16[4,32,1024]{2,1,0:T(8,128)(2,1)S(1)}, u32[]{:S(2)}, u32[]{:S(2)}) collective-permute-start(bf16[4,32,1024]{2,1,0:T(8,128)(2,1)S(1)} %pad_maximum_fusion.mine_ref), channel_id=1, source_target_pairs={{0,4},{4,0},{8,12},{12,8},{1,5},{5,1},{9,13},{13,9},{2,6},{6,2},{1... | collective-permute-start | bytes 786440 | tf_op jit(solution)/shard_map/ppermute | solution.py:365
  33.8 4.8 %copy-start.2 = (f32[3,2048]{1,0:T(4,128)S(1)}, f32[3,2048]{1,0:T(4,128)}, u32[]{:S(2)}) copy-start(f32[3,2048]{1,0:T(4,128)} %src_ref.1) | copy-start | bytes 73732
  46.4 1.8 %collective-permute-start.14 = (bf16[4,32,1024]{2,1,0:T(8,128)(2,1)S(1)}, bf16[4,32,1024]{2,1,0:T(8,128)(2,1)S(1)}, u32[]{:S(2)}, u32[]{:S(2)}) collective-permute-start(bf16[4,32,1024]{2,1,0:T(8,128)(2,1)S(1)} %collective-permute-done.11.refs_5_.refs_4_), channel_id=1, source_target_pairs={{0,16},{16,0},{1,17},{17,1},{2,18},{18,2},{3,19},{19,3},{4,20},{20... | collective-permute-start | bytes 786440 | tf_op jit(solution)/shard_map/ppermute | solution.py:365
  46.7 1.9 %collective-permute-start.13 = (bf16[4,32,1024]{2,1,0:T(8,128)(2,1)S(1)}, bf16[4,32,1024]{2,1,0:T(8,128)(2,1)S(1)}, u32[]{:S(2)}, u32[]{:S(2)}) collective-permute-start(bf16[4,32,1024]{2,1,0:T(8,128)(2,1)S(1)} %collective-permute-done.10.refs_4_.refs_5_), channel_id=1, source_target_pairs={{0,16},{16,0},{1,17},{17,1},{2,18},{18,2},{3,19},{19,3},{4,20},{20... | collective-permute-start | bytes 786440 | tf_op jit(solution)/shard_map/ppermute | solution.py:365
  47.2 1.8 %collective-permute-start.12 = (bf16[4,32,1024]{2,1,0:T(8,128)(2,1)S(1)}, bf16[4,32,1024]{2,1,0:T(8,128)(2,1)S(1)}, u32[]{:S(2)}, u32[]{:S(2)}) collective-permute-start(bf16[4,32,1024]{2,1,0:T(8,128)(2,1)S(1)} %collective-permute-done.9.refs_3_), channel_id=1, source_target_pairs={{0,16},{16,0},{1,17},{17,1},{2,18},{18,2},{3,19},{19,3},{4,20},{20... | collective-permute-start | bytes 786440 | tf_op jit(solution)/shard_map/ppermute | solution.py:365
  51.7 14.7 %collective-permute-start.17 = (f32[128,512]{1,0:T(8,128)S(1)}, f32[128,512]{1,0:T(8,128)S(1)}, u32[]{:S(2)}, u32[]{:S(2)}) collective-permute-start(f32[128,512]{1,0:T(8,128)S(1)} %leaf_sums.7), channel_id=1, source_target_pairs={{0,3},{1,0},{2,1},{3,2},{4,7},{5,4},{6,5},{7,6},{8,11},{9,8},{10,9... | collective-permute-start | bytes 786440 | tf_op jit(solution)/shard_map/ppermute | solution.py:361
  55.0 11.8 %collective-permute-start.16 = (f32[128,512]{1,0:T(8,128)S(1)}, f32[128,512]{1,0:T(8,128)S(1)}, u32[]{:S(2)}, u32[]{:S(2)}) collective-permute-start(f32[128,512]{1,0:T(8,128)S(1)} %leaf_sums.6), channel_id=1, source_target_pairs={{0,2},{1,3},{2,0},{3,1},{4,6},{5,7},{6,4},{7,5},{8,10},{9,11},{10,... | collective-permute-start | bytes 786440 | tf_op jit(solution)/shard_map/ppermute | solution.py:361
  60.4 10.0 %collective-permute-start.15 = (f32[128,512]{1,0:T(8,128)S(1)}, f32[128,512]{1,0:T(8,128)S(1)}, u32[]{:S(2)}, u32[]{:S(2)}) collective-permute-start(f32[128,512]{1,0:T(8,128)S(1)} %leaf_sums.5), channel_id=1, source_target_pairs={{0,1},{1,2},{2,3},{3,0},{4,5},{5,6},{6,7},{7,4},{8,9},{9,10},{10,1... | collective-permute-start | bytes 786440 | tf_op jit(solution)/shard_map/ppermute | solution.py:361
  74.2 5.3 %collective-permute-start.18 = (f32[128,128]{1,0:T(8,128)S(1)}, f32[128,128]{1,0:T(8,128)S(1)}, u32[]{:S(2)}, u32[]{:S(2)}) collective-permute-start(f32[128,128]{1,0:T(8,128)S(1)} %get-tuple-element.30.a_ref), channel_id=1, source_target_pairs={{0,1},{1,0},{2,3},{3,2},{4,5},{5,4},{6,7},{7,6},{8,9},{9,8},{10,11... | collective-permute-start | bytes 196616 | tf_op jit(solution)/shard_map/ppermute | solution.py:365
  82.8 5.9 %collective-permute-start.19 = (f32[128,128]{1,0:T(8,128)S(1)}, f32[128,128]{1,0:T(8,128)S(1)}, u32[]{:S(2)}, u32[]{:S(2)}) collective-permute-start(f32[128,128]{1,0:T(8,128)S(1)} %get-tuple-element.33.a_ref), channel_id=1, source_target_pairs={{0,2},{1,3},{2,0},{3,1},{4,6},{5,7},{6,4},{7,5},{8,10},{9,11},{10,... | collective-permute-start | bytes 196616 | tf_op jit(solution)/shard_map/ppermute | solution.py:365

commit v2 on v1

--- a/solution.py
+++ b/solution.py
@@ -57,17 +57,16 @@
 
 
 def tile_of(q, i, leaf, near_ref, src_ref, pts_ref, cols, centre):
-    _, c, x, y = place()
-    chunk = jnp.bitwise_and(2 * c + i, 3)
-    leaf_id = (jnp.bitwise_xor(x, q) * 4 + y) * 4 + chunk
+    _, _, x, y = place()
+    leaf_id = (jnp.bitwise_xor(x, q) * 4 + y) * 4 + i
     hit = near_ref[0, x * 4 + leaf] == leaf_id
     for k in range(1, 8):
         hit = jnp.logical_or(hit, near_ref[k, x * 4 + leaf] == leaf_id)
-    pts_ref[0:3, :] = src_ref[:, pl.ds(pl.multiple_of(chunk * LEAF, LEAF), LEAF)]
+    pts_ref[0:3, :] = src_ref[:, i * LEAF:(i + 1) * LEAF]
     return kernel_tile(features(pts_ref, centre, True, jnp.where(hit, 1e9, 0.0)), cols)
 
 
-def tiles_body(q, first, near_ref, tgt_ref, src_ref, out_ref, tpts_ref, spts_ref):
+def tiles_body(q, first, end, near_ref, tgt_ref, src_ref, out_ref, tpts_ref, spts_ref):
     _, _, x, y = place()
     spts_ref[...] = jnp.zeros_like(spts_ref)
 
@@ -79,18 +78,18 @@
                 q, i, leaf, near_ref, src_ref, spts_ref.at[i], cols, centre)
         return carry
 
-    lax.fori_loop(first, 4, one_leaf, 0)
+    lax.fori_loop(first, end, one_leaf, 0)
 
 
 def params():
     return pltpu.CompilerParams(vmem_limit_bytes=16 * 2**20)
 
 
-def kernel_tiles(q, first, near, targets, sources):
+def kernel_tiles(q, first, end, near, targets, sources):
     vm = pl.BlockSpec(memory_space=pltpu.VMEM)
     return pl.pallas_call(
-        functools.partial(tiles_body, q, first),
-        out_shape=jax.ShapeDtypeStruct((4 - first, 2048, LEAF), BF),
+        functools.partial(tiles_body, q, first, end),
+        out_shape=jax.ShapeDtypeStruct((end - first, 2048, LEAF), BF),
         in_specs=[pl.BlockSpec(memory_space=pltpu.SMEM), vm, vm],
         out_specs=vm,
         scratch_shapes=[pltpu.VMEM((8, LEAF), F32), pltpu.VMEM((4, 8, LEAF), F32)],
@@ -108,11 +107,13 @@
         leaf = jnp.bitwise_and(y + turn, 3)
         cols, centre = target_features(tgt_ref, tpts_ref, x * 4 + leaf)
         total = None
-        for n, rows_ref in enumerate((mine_ref, other_ref)):
+        for n in range(2):
             for i in (2 * n, 2 * n + 1):
                 held_ref[i * LEAF:(i + 1) * LEAF, :] = tile_of(
                     0, i, leaf, near_ref, src_ref, spts_ref.at[i], cols, centre)
-            term = jnp.dot(rows_ref[...].reshape(128, 1024), held_ref[1024 * n:1024 * (n + 1), :], preferred_element_type=F32)
+            part = slice(1024 * n, 1024 * (n + 1))
+            rows = jnp.concatenate([r[:, :, part].reshape(64, 1024) for r in (mine_ref, other_ref)], axis=0)
+            term = jnp.dot(rows, held_ref[part, :], preferred_element_type=F32)
             total = term if total is None else total + term
         out_ref[turn] = total
         return carry
@@ -134,7 +135,7 @@
     )(near, targets, sources, mine, other)
 
 
-def sums_body(turn, stored, fused, near_ref, tgt_ref, base_ref, *refs):
+def sums_body(turn, stored, fused, places, near_ref, tgt_ref, base_ref, *refs):
     ns, nf = len(stored), len(fused)
     tiles, refs = refs[:ns], refs[ns:]
     srcs, refs = refs[:nf], refs[nf:]
@@ -147,14 +148,14 @@
     spts_ref[...] = jnp.zeros_like(spts_ref)
     total = base_ref[turn]
     for n in range(ns + nf):
-        rows = jnp.concatenate([mine[n][...].reshape(128, 1024), other[n][...].reshape(128, 1024)], axis=1)
+        rows = jnp.concatenate([mine[n][...].reshape(64, 2048), other[n][...].reshape(64, 2048)], axis=0)
         if n >= ns:
             for i in range(4):
                 held_ref[n - ns, i * LEAF:(i + 1) * LEAF, :] = tile_of(
                     fused[n - ns], i, leaf, near_ref, srcs[n - ns], spts_ref.at[4 * (n - ns) + i], cols, centre)
             tile = held_ref[n - ns]
         else:
-            tile = tiles[n][turn - 4 + tiles[n].shape[0]]
+            tile = tiles[n][places[n]]
         total = total + jnp.dot(rows, tile, preferred_element_type=F32)
     out_ref[...] = total
 
@@ -165,7 +166,7 @@
     vm = pl.BlockSpec(memory_space=pltpu.VMEM)
     sm = pl.BlockSpec(memory_space=pltpu.SMEM)
     return pl.pallas_call(
-        functools.partial(sums_body, turn, stored, fused),
+        functools.partial(sums_body, turn, stored, fused, [tiles[q][1] for q in stored]),
         out_shape=jax.ShapeDtypeStruct((128, LEAF), F32),
         in_specs=[sm, vm, vm] + [vm] * (3 * (len(stored) + len(fused))),
         scratch_shapes=[
@@ -176,7 +177,7 @@
         cost_estimate=pl.CostEstimate(flops=4_000_000_000, bytes_accessed=9_000_000, transcendentals=1_000_000),
         compiler_params=params(),
         name="leaf_sums",
-    )(near, targets, base, *[tiles[q] for q in stored], *[sources[q] for q in fused],
+    )(near, targets, base, *[tiles[q][0] for q in stored], *[sources[q] for q in fused],
       *[mine[q] for q in order], *[other[q] for q in order])
 
 
@@ -282,10 +283,11 @@
 
 
 def leaf_body(a_ref, b_ref, c_ref, d_ref, z_ref, inv_ref, proj_ref, sq_ref, aug_ref, top_ref):
+    z, c, _, _ = place()
     for k in range(4):
         for s in range(2):
-            plane = jnp.bitwise_xor(jnp.bitwise_and(place()[0] - 2 * k, 7), s)
-            rows = slice(16 * (2 * k + s), 16 * (2 * k + s) + 16)
+            plane = jnp.bitwise_and(z - 2 * k - (c if s == 0 else 1 - c), 7)
+            rows = slice(64 * s + 16 * k, 64 * s + 16 * k + 16)
             both = (a_ref[rows, :] + b_ref[rows, :]) + (c_ref[rows, :] + d_ref[rows, :])
             z_ref[pl.ds(pl.multiple_of(plane * 16, 16), 16), :] = both
     z = z_ref[...]
@@ -365,19 +367,18 @@
     return lax.ppermute(x, axis, [(i, i ^ bit) for i in range(lax.axis_size(axis))])
 
 
-def diagonal(x):
-    return lax.ppermute(x, ROW, [(i, i ^ 3) for i in range(16)])
-
-
-def own_pair(samples, core):
+def over_planes(x, even, odd):
+    pairs = [(2 * i + c, 2 * ((i + by) % 8) + c) for i in range(8) for c, by in ((0, even), (1, odd)) if by]
+    return lax.ppermute(x, ROW, pairs)
+
+
+def own_planes(samples, core):
     flat = samples.T
-    half = flat.shape[1] // 2
-    mine = lax.dynamic_slice_in_dim(flat, core * half, half, 1)
-    away = lax.dynamic_slice_in_dim(flat, (1 - core) * half, half, 1)
-    across, up, cross = crossed(away, "c", 1), crossed(mine, "z", 1), diagonal(away)
-    first = jnp.where(core == 0, jnp.concatenate([mine, across]), jnp.concatenate([across, mine]))
-    second = jnp.where(core == 0, jnp.concatenate([up, cross]), jnp.concatenate([cross, up]))
-    return jnp.concatenate([first, second])
+    across = crossed(flat, "c", 1)
+    own = jnp.where(core == 0, jnp.concatenate([flat, across]), jnp.concatenate([across, flat]))
+    behind = [over_planes(own, 2 * k, 2 * k + 1) for k in (1, 2, 3)]
+    first = jnp.where(core == 0, own, over_planes(own, None, 1))
+    return own, jnp.stack([first] + behind)
 
 
 def after(x, *work):
@@ -388,21 +389,27 @@
     core = lax.axis_index("c")
     near = near.T
     beside = crossed(sources, "x", 1)
-    pair = own_pair(samples, core)
-    block = jnp.stack([pair] + [moved(pair, "z", 2 * k) for k in (1, 2, 3)])
+    own, block = own_planes(samples, core)
+    beside = after(beside, own)
     behind = crossed(jnp.stack([sources, beside]), "x", 2)
-    tiles = {1: kernel_tiles(1, 0, near, targets, after(beside, pair))}
-    block = after(block, tiles[1])
+    early = kernel_tiles(1, 0, 4, near, targets, beside)
+    block = after(block, early)
     sent = {q: crossed(block, "x", q) for q in (2, 1, 3)}
     swapped = crossed(block, "c", 1)
-    tiles[3] = kernel_tiles(3, 1, near, targets, after(behind[1], swapped))
-    base = own_sums(near, targets, sources, block, after(swapped, tiles[3]))
+    middle = kernel_tiles(3, 1, 3, near, targets, after(behind[1], swapped))
+    base = own_sums(near, targets, sources, block, after(swapped, middle))
     mine = {q: after(b, base) for q, b in sent.items()}
-    other = {q: crossed(b, "c", 1) for q, b in mine.items()}
-    sums = {}
+    other, sums = {}, {}
+    for q, b in mine.items():
+        other[q] = crossed(b, "c", 1)
+    late = kernel_tiles(3, 3, 4, near, targets, behind[1])
     for d in (2, 1, 3, 0):
-        made = tiles if d else {1: tiles[1]}
-        fused = {2: behind[0]} if d else {2: behind[0], 3: behind[1]}
+        made = {1: (early, d)}
+        fused = {2: behind[0]}
+        if d:
+            made[3] = (late, 0) if d == 3 else (middle, d - 1)
+        else:
+            fused[3] = behind[1]
         part = leaf_sums(d, near, targets, base, made, fused, mine, other)
         sums[d] = moved(part, "y", d) if d else part
     far_sample, inv0, proj0, sq0 = leaf_node([sums[d] for d in range(4)])

time: 93.7 us -> 90.6 us (0.967)
  starting transfers between devices: 32.2 us -> 27.4 us
  waiting for transfers between devices: 12.1 us -> 13.6 us
    ppermute x6 -> x3, starting transfers between devices: 15.9 us -> 5.38 us  [moved(): return lax.ppermute(x, axis, [(i, (i + by) % size) for i in range(size)])]
    ppermute x1 -> x4, starting transfers between devices: 2.03 us -> 10.8 us  [over_planes(): return lax.ppermute(x, ROW, pairs)]
    ppermute x13 -> x12, starting transfers between devices: 14.3 us -> 11.2 us  [crossed(): lax.ppermute(x, axis, [(i, i ^ bit) for i in range(lax.axis_size(axis))])]
    ppermute x6 -> x3, waiting for transfers between devices: 3.9 us -> 5.26 us  [moved(): return lax.ppermute(x, axis, [(i, (i + by) % size) for i in range(size)])]
    pallas_call x6 -> x7, Pallas kernels: 23.1 us -> 23.8 us  [the longest x4 12.1 us: leaf_sums(): pl.pallas_call(functools.partial(sums_body, turn, stored, fused, [tiles[q...]
    ppermute x13 -> x12, waiting for transfers between devices: 8.15 us -> 8.33 us  [crossed(): lax.ppermute(x, axis, [(i, i ^ bit) for i in range(lax.axis_size(axis))])]
  transfers between devices with their start and end apart: 20 -> 19, of which waited for: 8 -> 5; matrix products, arithmetic and copies ran while one was open for 1% -> 2% of each run, Pallas kernels for 33% -> 34%
where the time goes in v2:
time: 90.6 us; the launch traced here: 90.3 us
  Pallas kernels  45.1 us (50%)
  starting transfers between devices  27.4 us (30%)
  waiting for transfers between devices  13.6 us (15%)
  other arithmetic  1.69 us (2%)
  local copies, waits for them, and re-layouts  1.61 us (2%)
    pallas_call x4, Pallas kernels, leaf_sums(): pl.pallas_call(functools.partial(sums_body, turn, stored, fused, [tiles[q...  12.1 us
    pallas_call x3, Pallas kernels, kernel_tiles(): pl.pallas_call(functools.partial(tiles_body, q, first, end), out_shape=ja...  11.7 us
    ppermute x12, starting transfers between devices, crossed(): lax.ppermute(x, axis, [(i, i ^ bit) for i in range(lax.axis_size(axis))])  11.2 us
    ppermute x4, starting transfers between devices, over_planes(): return lax.ppermute(x, ROW, pairs)  10.8 us
    ppermute x12, waiting for transfers between devices, crossed(): lax.ppermute(x, axis, [(i, i ^ bit) for i in range(lax.axis_size(axis))])  8.33 us
    pallas_call x1, Pallas kernels, own_sums(): pl.pallas_call(own_body, out_shape=jax.ShapeDtypeStruct((4, 128, LEAF), F...  7.75 us
    ppermute x3, starting transfers between devices, moved(): return lax.ppermute(x, axis, [(i, (i + by) % size) for i in range(size)])  5.38 us
    ppermute x3, waiting for transfers between devices, moved(): return lax.ppermute(x, axis, [(i, (i + by) % size) for i in range(size)])  5.26 us
  transfers between devices with their start and end apart: 19, of which 5 were waited for; matrix products, arithmetic and copies ran while one was open for 2% of the time, Pallas kernels for 34%

profile of v2, /device:TPU:8, one launch (start us, length us, event | category | flops | bytes accessed | tf_op | source)
XLA Modules:
  0.0 90.3 jit_solution(11684706678270543606)
XLA Ops:
  0.7 1.6 %collective-permute-start.5 = (f32[3,2048]{1,0:T(4,128)}, f32[3,2048]{1,0:T(4,128)S(1)}, u32[]{:S(2)}, u32[]{:S(2)}) collective-permute-start(f32[3,2048]{1,0:T(4,128)} %src_ref.1), channel_id=1, source_target_pairs={{0,4},{4,0},{8,12},{12,8},{1,5},{5,1},{9,13},{13,9},{2,6},{6,2},{1... | collective-permute-start | bytes 73736 | tf_op jit(solution)/shard_map/ppermute | solution.py:367
  2.3 0.8 maximum_select_fusion
  3.2 6.4 %collective-permute-start.4 = (bf16[16,2048]{1,0:T(8,128)(2,1)S(1)}, bf16[16,2048]{1,0:T(8,128)(2,1)S(1)}, u32[]{:S(2)}, u32[]{:S(2)}) collective-permute-start(bf16[16,2048]{1,0:T(8,128)(2,1)S(1)} %maximum_select_fusion), channel_id=1, source_target_pairs={{0,192},{16,240},{32,224},{48,16},{64,0},{80,48},{96,32},{112,80},... | collective-permute-start | bytes 196616 | tf_op jit(solution)/shard_map/ppermute | solution.py:372
  9.5 1.0 %collective-permute-start.3 = (bf16[16,2048]{1,0:T(8,128)(2,1)S(1)}, bf16[16,2048]{1,0:T(8,128)(2,1)S(1)}, u32[]{:S(2)}, u32[]{:S(2)}) collective-permute-start(bf16[16,2048]{1,0:T(8,128)(2,1)S(1)} %maximum_select_fusion), channel_id=1, source_target_pairs={{0,128},{16,176},{32,160},{48,208},{64,192},{80,240},{96,224},{112... | collective-permute-start | bytes 196616 | tf_op jit(solution)/shard_map/ppermute | solution.py:372
  10.5 2.8 %collective-permute-start.2 = (bf16[16,2048]{1,0:T(8,128)(2,1)S(1)}, bf16[16,2048]{1,0:T(8,128)(2,1)S(1)}, u32[]{:S(2)}, u32[]{:S(2)}) collective-permute-start(bf16[16,2048]{1,0:T(8,128)(2,1)S(1)} %maximum_select_fusion), channel_id=1, source_target_pairs={{0,64},{16,112},{32,96},{48,144},{64,128},{80,176},{96,160},{112,2... | collective-permute-start | bytes 196616 | tf_op jit(solution)/shard_map/ppermute | solution.py:372
  14.0 0.8 pad_maximum_fusion.1
  14.8 2.9 %collective-permute-start.7 = (f32[2,3,2048]{2,1,0:T(4,128)S(1)}, f32[2,3,2048]{2,1,0:T(4,128)S(1)}, u32[]{:S(2)}, u32[]{:S(2)}) collective-permute-start(f32[2,3,2048]{2,1,0:T(4,128)S(1)} %pad_maximum_fusion.1), channel_id=1, source_target_pairs={{0,8},{4,12},{8,0},{12,4},{1,9},{5,13},{9,1},{13,5},{2,10},{6,14},... | collective-permute-start | bytes 147464 | tf_op jit(solution)/shard_map/ppermute | solution.py:367
  17.7 0.9 copy-done
  18.6 0.7 copy-done.2
  19.3 6.2 %kernel_tiles.3.refs_0_ = bf16[4,2048,512]{2,1,0:T(8,128)(2,1)S(1)} custom-call(s32[8,16]{1,0:T(8,128)S(1)} %bitcast.15, f32[3,8192]{1,0:T(4,128)S(1)} %copy-done, f32[3,2048]{1,0:T(4,128)S(1)} %collective-permute-done.5.src_ref), custom_call_target="tpu_custom_call" | custom-call | flops 8000000000 | bytes 8400000 | tf_op jit(solution)/shard_map/kernel_tiles/pallas_call | solution.py:90
  26.5 2.0 %collective-permute-start.9 = (bf16[4,16,2048]{2,1,0:T(8,128)(2,1)S(1)}, bf16[4,16,2048]{2,1,0:T(8,128)(2,1)S(1)}, u32[]{:S(2)}, u32[]{:S(2)}) collective-permute-start(bf16[4,16,2048]{2,1,0:T(8,128)(2,1)S(1)} %pad_maximum_fusion.mine_ref), channel_id=1, source_target_pairs={{0,8},{4,12},{8,0},{12,4},{1,9},{5,13},{9,1},{13,5},{2,10},{6,14},... | collective-permute-start | bytes 786440 | tf_op jit(solution)/shard_map/ppermute | solution.py:367
  28.5 2.1 %collective-permute-start.10 = (bf16[4,16,2048]{2,1,0:T(8,128)(2,1)S(1)}, bf16[4,16,2048]{2,1,0:T(8,128)(2,1)S(1)}, u32[]{:S(2)}, u32[]{:S(2)}) collective-permute-start(bf16[4,16,2048]{2,1,0:T(8,128)(2,1)S(1)} %pad_maximum_fusion.mine_ref), channel_id=1, source_target_pairs={{0,12},{4,8},{8,4},{12,0},{1,13},{5,9},{9,5},{13,1},{2,14},{6,10},... | collective-permute-start | bytes 786440 | tf_op jit(solution)/shard_map/ppermute | solution.py:367
  30.6 3.4 %kernel_tiles.4.refs_1_ = bf16[2,2048,512]{2,1,0:T(8,128)(2,1)S(1)} custom-call(s32[8,16]{1,0:T(8,128)S(1)} %bitcast.16, f32[3,8192]{1,0:T(4,128)S(1)} %copy-done, f32[3,2048]{1,0:T(4,128)S(1)} %get-tuple-element.21.src_ref.refs_2_), custom_call_target="tpu_custom_call" | custom-call | flops 8000000000 | bytes 8400000 | tf_op jit(solution)/shard_map/kernel_tiles/pallas_call | solution.py:90
  34.1 7.8 %own_sums.1.base_ref = f32[4,128,512]{2,1,0:T(8,128)S(1)} custom-call(s32[8,16]{1,0:T(8,128)S(1)} %bitcast.17, f32[3,8192]{1,0:T(4,128)S(1)} %copy-done, f32[3,2048]{1,0:T(4,128)S(1)} %copy-done.1, bf16[4,16,2048]{2,1,0:T(8,128)(2,1)S(1)} %pad_maximum_fusion.mine_ref, bf16[4,16,2048]{2,1,0:T(8,128)(2,1)S(1)} %collective-permute-done.6.other_ref), custom_call_target="tpu_custom_call" | custom-call | flops 8000000000 | bytes 8400000 | tf_op jit(solution)/shard_map/own_sums/pallas_call | solution.py:126
  41.9 1.6 %collective-permute-done.10.refs_5_.refs_4_ = bf16[4,16,2048]{2,1,0:T(8,128)(2,1)S(1)} collective-permute-done((bf16[4,16,2048]{2,1,0:T(8,128)(2,1)S(1)}, bf16[4,16,2048]{2,1,0:T(8,128)(2,1)S(1)}, u32[]{:S(2)}, u32[]{:S(2)}) %collective-permute-start.10) | collective-permute-done | bytes 262176 | tf_op jit(solution)/shard_map/ppermute | solution.py:367
  44.0 2.0 %kernel_tiles.5.refs_1_ = bf16[1,2048,512]{2,1,0:T(8,128)(2,1)S(1)} custom-call(s32[8,16]{1,0:T(8,128)S(1)} %bitcast.18, f32[3,8192]{1,0:T(4,128)S(1)} %copy-done, f32[3,2048]{1,0:T(4,128)S(1)} %get-tuple-element.21.src_ref.refs_2_), custom_call_target="tpu_custom_call" | custom-call | flops 8000000000 | bytes 8400000 | tf_op jit(solution)/shard_map/kernel_tiles/pallas_call | solution.py:90
  46.1 2.7 %leaf_sums.5 = f32[128,512]{1,0:T(8,128)S(1)} custom-call(s32[8,16]{1,0:T(8,128)S(1)} %bitcast.19, f32[3,8192]{1,0:T(4,128)S(1)} %copy-done, f32[4,128,512]{2,1,0:T(8,128)S(1)} %own_sums.1.base_ref, bf16[4,2048,512]{2,1,0:T(8,128)(2,1)S(1)} %kernel_tiles.3.refs_0_, bf16[2,2048,512]{2,1,0:T(8,128)(2,1)S(1)} %kernel_tiles.4.refs_1_, ...), custom_call_target="tpu_custom_call" | custom-call | flops 4000000000 | bytes 9000000 | tf_op jit(solution)/shard_map/leaf_sums/pallas_call | solution.py:168
  48.8 1.6 %collective-permute-start.14 = (f32[128,512]{1,0:T(8,128)S(1)}, f32[128,512]{1,0:T(8,128)S(1)}, u32[]{:S(2)}, u32[]{:S(2)}) collective-permute-start(f32[128,512]{1,0:T(8,128)S(1)} %leaf_sums.5), channel_id=1, source_target_pairs={{0,1},{1,2},{2,3},{3,0},{4,5},{5,6},{6,7},{7,4},{8,9},{9,10},{10,1... | collective-permute-start | bytes 786440 | tf_op jit(solution)/shard_map/ppermute | solution.py:363
  50.4 2.7 %leaf_sums.6 = f32[128,512]{1,0:T(8,128)S(1)} custom-call(s32[8,16]{1,0:T(8,128)S(1)} %bitcast.20, f32[3,8192]{1,0:T(4,128)S(1)} %copy-done, f32[4,128,512]{2,1,0:T(8,128)S(1)} %own_sums.1.base_ref, bf16[4,2048,512]{2,1,0:T(8,128)(2,1)S(1)} %kernel_tiles.3.refs_0_, bf16[2,2048,512]{2,1,0:T(8,128)(2,1)S(1)} %kernel_tiles.4.refs_1_, ...), custom_call_target="tpu_custom_call" | custom-call | flops 4000000000 | bytes 9000000 | tf_op jit(solution)/shard_map/leaf_sums/pallas_call | solution.py:168
  53.2 1.0 %collective-permute-start.15 = (f32[128,512]{1,0:T(8,128)S(1)}, f32[128,512]{1,0:T(8,128)S(1)}, u32[]{:S(2)}, u32[]{:S(2)}) collective-permute-start(f32[128,512]{1,0:T(8,128)S(1)} %leaf_sums.6), channel_id=1, source_target_pairs={{0,2},{1,3},{2,0},{3,1},{4,6},{5,7},{6,4},{7,5},{8,10},{9,11},{10,... | collective-permute-start | bytes 786440 | tf_op jit(solution)/shard_map/ppermute | solution.py:363
  54.2 2.7 %leaf_sums.7 = f32[128,512]{1,0:T(8,128)S(1)} custom-call(s32[8,16]{1,0:T(8,128)S(1)} %bitcast.21, f32[3,8192]{1,0:T(4,128)S(1)} %copy-done, f32[4,128,512]{2,1,0:T(8,128)S(1)} %own_sums.1.base_ref, bf16[4,2048,512]{2,1,0:T(8,128)(2,1)S(1)} %kernel_tiles.3.refs_0_, bf16[1,2048,512]{2,1,0:T(8,128)(2,1)S(1)} %kernel_tiles.5.refs_1_, ...), custom_call_target="tpu_custom_call" | custom-call | flops 4000000000 | bytes 9000000 | tf_op jit(solution)/shard_map/leaf_sums/pallas_call | solution.py:168
  56.9 2.7 %collective-permute-start.16 = (f32[128,512]{1,0:T(8,128)S(1)}, f32[128,512]{1,0:T(8,128)S(1)}, u32[]{:S(2)}, u32[]{:S(2)}) collective-permute-start(f32[128,512]{1,0:T(8,128)S(1)} %leaf_sums.7), channel_id=1, source_target_pairs={{0,3},{1,0},{2,1},{3,2},{4,7},{5,4},{6,5},{7,6},{8,11},{9,8},{10,9... | collective-permute-start | bytes 786440 | tf_op jit(solution)/shard_map/ppermute | solution.py:363
  59.6 3.9 %leaf_sums.4.a_ref = f32[128,512]{1,0:T(8,128)S(1)} custom-call(s32[8,16]{1,0:T(8,128)S(1)} %bitcast.22, f32[3,8192]{1,0:T(4,128)S(1)} %copy-done, f32[4,128,512]{2,1,0:T(8,128)S(1)} %own_sums.1.base_ref, bf16[4,2048,512]{2,1,0:T(8,128)(2,1)S(1)} %kernel_tiles.3.refs_0_, f32[3,2048]{1,0:T(4,128)S(1)} %get-tuple-element.36.refs_1_.refs_2_, ...), custom_call_target="tpu_custom_call" | custom-call | flops 4000000000 | bytes 9000000 | tf_op jit(solution)/shard_map/leaf_sums/pallas_call | solution.py:168
  64.0 4.8 %collective-permute-done.16.d_ref = f32[128,512]{1,0:T(8,128)S(1)} collective-permute-done((f32[128,512]{1,0:T(8,128)S(1)}, f32[128,512]{1,0:T(8,128)S(1)}, u32[]{:S(2)}, u32[]{:S(2)}) %collective-permute-start.16) | collective-permute-done | bytes 262176 | tf_op jit(solution)/shard_map/ppermute | solution.py:363
  68.8 3.9 %leaf_node.1 = (f32[128,512]{1,0:T(8,128)S(1)}, f32[128,128]{1,0:T(8,128)S(1)}, f32[128,128]{1,0:T(8,128)S(1)}, f32[128,128]{1,0:T(8,128)S(1)}) custom-call(f32[128,512]{1,0:T(8,128)S(1)} %leaf_sums.4.a_ref, f32[128,512]{1,0:T(8,128)S(1)} %collective-permute-done.14.b_ref, f32[128,512]{1,0:T(8,128)S(1)} %collective-permute-done.15.c_ref, ...), custom_call_target="tpu_custom_call" | custom-call | tf_op jit(solution)/shard_map/leaf_node/pallas_call | solution.py:331
  72.8 1.3 %carry.1 = (f32[512,128]{1,0:T(8,128)}, f32[512,128]{1,0:T(8,128)S(1)}) custom-call(f32[128,512]{1,0:T(8,128)S(1)} %get-tuple-element.26.z_ref, f32[128,128]{1,0:T(8,128)S(1)} %get-tuple-element.27.inv_ref, f32[128,128]{1,0:T(8,128)S(1)} %get-tuple-element.28.proj_ref), custom_call_target="tpu_custom_call" | custom-call | tf_op jit(solution)/shard_map/carry/pallas_call | solution.py:346
  74.1 2.9 %collective-permute-done.17.b_ref = f32[128,128]{1,0:T(8,128)S(1)} collective-permute-done((f32[128,128]{1,0:T(8,128)S(1)}, f32[128,128]{1,0:T(8,128)S(1)}, u32[]{:S(2)}, u32[]{:S(2)}) %collective-permute-start.17) | collective-permute-done | bytes 65568 | tf_op jit(solution)/shard_map/ppermute | solution.py:367
  77.0 3.3 %pair_node.1 = (f32[128,128]{1,0:T(8,128)S(1)}, f32[128,128]{1,0:T(8,128)S(1)}, f32[128,128]{1,0:T(8,128)S(1)}) custom-call(f32[128,128]{1,0:T(8,128)S(1)} %get-tuple-element.30.a_ref, f32[128,128]{1,0:T(8,128)S(1)} %collective-permute-done.17.b_ref), custom_call_target="tpu_custom_call" | custom-call | tf_op jit(solution)/shard_map/pair_node/pallas_call | solution.py:342
  80.3 1.1 %collective-permute-start.18 = (f32[128,128]{1,0:T(8,128)S(1)}, f32[128,128]{1,0:T(8,128)S(1)}, u32[]{:S(2)}, u32[]{:S(2)}) collective-permute-start(f32[128,128]{1,0:T(8,128)S(1)} %get-tuple-element.33.a_ref), channel_id=1, source_target_pairs={{0,2},{1,3},{2,0},{3,1},{4,6},{5,7},{6,4},{7,5},{8,10},{9,11},{10,... | collective-permute-start | bytes 196616 | tf_op jit(solution)/shard_map/ppermute | solution.py:367
  81.4 1.0 %carry2.1.z_ref = f32[512,128]{1,0:T(8,128)S(1)} custom-call(f32[512,128]{1,0:T(8,128)S(1)} %get-tuple-element.31.z_ref, f32[128,128]{1,0:T(8,128)S(1)} %get-tuple-element.34.inv_ref, f32[128,128]{1,0:T(8,128)S(1)} %get-tuple-element.35.proj_ref), custom_call_target="tpu_custom_call" | custom-call | tf_op jit(solution)/shard_map/carry2/pallas_call | solution.py:350
  82.5 3.7 %collective-permute-done.18.b_ref = f32[128,128]{1,0:T(8,128)S(1)} collective-permute-done((f32[128,128]{1,0:T(8,128)S(1)}, f32[128,128]{1,0:T(8,128)S(1)}, u32[]{:S(2)}, u32[]{:S(2)}) %collective-permute-start.18) | collective-permute-done | bytes 65568 | tf_op jit(solution)/shard_map/ppermute | solution.py:367
  86.2 4.1 %last_node.1 = f32[512,128]{1,0:T(8,128)} custom-call(f32[128,128]{1,0:T(8,128)S(1)} %get-tuple-element.33.a_ref, f32[128,128]{1,0:T(8,128)S(1)} %collective-permute-done.18.b_ref, f32[512,128]{1,0:T(8,128)S(1)} %carry2.1.z_ref), custom_call_target="tpu_custom_call" | custom-call | tf_op jit(solution)/shard_map/last_node/pallas_call | solution.py:354
  (32 shorter events, 2.7 us)
Async XLA Ops:
  0.6 1.7 %collective-permute-start = (bf16[8,2048]{1,0:T(8,128)(2,1)}, bf16[8,2048]{1,0:T(8,128)(2,1)S(1)}, u32[]{:S(2)}, u32[]{:S(2)}) collective-permute-start(bf16[8,2048]{1,0:T(8,128)(2,1)} %bitcast.23), channel_id=1, source_target_pairs={{0,16},{16,0},{1,17},{17,1},{2,18},{18,2},{3,19},{19,3},{4,20},{20... | collective-permute-start | bytes 98312 | tf_op jit(solution)/shard_map/ppermute | solution.py:367
  0.7 13.3 %collective-permute-start.5 = (f32[3,2048]{1,0:T(4,128)}, f32[3,2048]{1,0:T(4,128)S(1)}, u32[]{:S(2)}, u32[]{:S(2)}) collective-permute-start(f32[3,2048]{1,0:T(4,128)} %src_ref.1), channel_id=1, source_target_pairs={{0,4},{4,0},{8,12},{12,8},{1,5},{5,1},{9,13},{13,9},{2,6},{6,2},{1... | collective-permute-start | bytes 73736 | tf_op jit(solution)/shard_map/ppermute | solution.py:367
  3.2 22.5 %collective-permute-start.4 = (bf16[16,2048]{1,0:T(8,128)(2,1)S(1)}, bf16[16,2048]{1,0:T(8,128)(2,1)S(1)}, u32[]{:S(2)}, u32[]{:S(2)}) collective-permute-start(bf16[16,2048]{1,0:T(8,128)(2,1)S(1)} %maximum_select_fusion), channel_id=1, source_target_pairs={{0,192},{16,240},{32,224},{48,16},{64,0},{80,48},{96,32},{112,80},... | collective-permute-start | bytes 196616 | tf_op jit(solution)/shard_map/ppermute | solution.py:372
  9.5 16.1 %collective-permute-start.3 = (bf16[16,2048]{1,0:T(8,128)(2,1)S(1)}, bf16[16,2048]{1,0:T(8,128)(2,1)S(1)}, u32[]{:S(2)}, u32[]{:S(2)}) collective-permute-start(bf16[16,2048]{1,0:T(8,128)(2,1)S(1)} %maximum_select_fusion), channel_id=1, source_target_pairs={{0,128},{16,176},{32,160},{48,208},{64,192},{80,240},{96,224},{112... | collective-permute-start | bytes 196616 | tf_op jit(solution)/shard_map/ppermute | solution.py:372
  10.5 15.1 %collective-permute-start.2 = (bf16[16,2048]{1,0:T(8,128)(2,1)S(1)}, bf16[16,2048]{1,0:T(8,128)(2,1)S(1)}, u32[]{:S(2)}, u32[]{:S(2)}) collective-permute-start(bf16[16,2048]{1,0:T(8,128)(2,1)S(1)} %maximum_select_fusion), channel_id=1, source_target_pairs={{0,64},{16,112},{32,96},{48,144},{64,128},{80,176},{96,160},{112,2... | collective-permute-start | bytes 196616 | tf_op jit(solution)/shard_map/ppermute | solution.py:372
  13.4 12.2 %collective-permute-start.1 = (bf16[16,2048]{1,0:T(8,128)(2,1)S(1)}, bf16[16,2048]{1,0:T(8,128)(2,1)S(1)}, u32[]{:S(2)}, u32[]{:S(2)}) collective-permute-start(bf16[16,2048]{1,0:T(8,128)(2,1)S(1)} %maximum_select_fusion), channel_id=1, source_target_pairs={{16,48},{48,80},{80,112},{112,144},{144,176},{176,208},{208,240},{... | collective-permute-start | bytes 196616 | tf_op jit(solution)/shard_map/ppermute | solution.py:372
  14.8 11.0 %collective-permute-start.7 = (f32[2,3,2048]{2,1,0:T(4,128)S(1)}, f32[2,3,2048]{2,1,0:T(4,128)S(1)}, u32[]{:S(2)}, u32[]{:S(2)}) collective-permute-start(f32[2,3,2048]{2,1,0:T(4,128)S(1)} %pad_maximum_fusion.1), channel_id=1, source_target_pairs={{0,8},{4,12},{8,0},{12,4},{1,9},{5,13},{9,1},{13,5},{2,10},{6,14},... | collective-permute-start | bytes 147464 | tf_op jit(solution)/shard_map/ppermute | solution.py:367
  17.7 0.9 %copy-start = (f32[3,8192]{1,0:T(4,128)S(1)}, f32[3,8192]{1,0:T(4,128)}, u32[]{:S(2)}) copy-start(f32[3,8192]{1,0:T(4,128)} %tgt_ref.15) | copy-start | bytes 294916
  18.6 0.7 copy-start.2
  19.3 6.3 %copy-start.3 = (bf16[2048,8]{0,1:T(8,128)(2,1)S(1)}, bf16[2048,8]{0,1:T(8,128)(2,1)}, u32[]{:S(2)}) copy-start(bf16[2048,8]{0,1:T(8,128)(2,1)} %param.6) | copy-start | bytes 98308
  25.7 4.9 %collective-permute-start.6 = (bf16[4,16,2048]{2,1,0:T(8,128)(2,1)S(1)}, bf16[4,16,2048]{2,1,0:T(8,128)(2,1)S(1)}, u32[]{:S(2)}, u32[]{:S(2)}) collective-permute-start(bf16[4,16,2048]{2,1,0:T(8,128)(2,1)S(1)} %pad_maximum_fusion.mine_ref), channel_id=1, source_target_pairs={{0,16},{16,0},{1,17},{17,1},{2,18},{18,2},{3,19},{19,3},{4,20},{20... | collective-permute-start | bytes 786440 | tf_op jit(solution)/shard_map/ppermute | solution.py:367
  25.9 16.0 %collective-permute-start.8 = (bf16[4,16,2048]{2,1,0:T(8,128)(2,1)S(1)}, bf16[4,16,2048]{2,1,0:T(8,128)(2,1)S(1)}, u32[]{:S(2)}, u32[]{:S(2)}) collective-permute-start(bf16[4,16,2048]{2,1,0:T(8,128)(2,1)S(1)} %pad_maximum_fusion.mine_ref), channel_id=1, source_target_pairs={{0,4},{4,0},{8,12},{12,8},{1,5},{5,1},{9,13},{13,9},{2,6},{6,2},{1... | collective-permute-start | bytes 786440 | tf_op jit(solution)/shard_map/ppermute | solution.py:367
  26.5 15.4 %collective-permute-start.9 = (bf16[4,16,2048]{2,1,0:T(8,128)(2,1)S(1)}, bf16[4,16,2048]{2,1,0:T(8,128)(2,1)S(1)}, u32[]{:S(2)}, u32[]{:S(2)}) collective-permute-start(bf16[4,16,2048]{2,1,0:T(8,128)(2,1)S(1)} %pad_maximum_fusion.mine_ref), channel_id=1, source_target_pairs={{0,8},{4,12},{8,0},{12,4},{1,9},{5,13},{9,1},{13,5},{2,10},{6,14},... | collective-permute-start | bytes 786440 | tf_op jit(solution)/shard_map/ppermute | solution.py:367
  28.5 15.0 %collective-permute-start.10 = (bf16[4,16,2048]{2,1,0:T(8,128)(2,1)S(1)}, bf16[4,16,2048]{2,1,0:T(8,128)(2,1)S(1)}, u32[]{:S(2)}, u32[]{:S(2)}) collective-permute-start(bf16[4,16,2048]{2,1,0:T(8,128)(2,1)S(1)} %pad_maximum_fusion.mine_ref), channel_id=1, source_target_pairs={{0,12},{4,8},{8,4},{12,0},{1,13},{5,9},{9,5},{13,1},{2,14},{6,10},... | collective-permute-start | bytes 786440 | tf_op jit(solution)/shard_map/ppermute | solution.py:367
  30.6 3.4 %copy-start.1 = (f32[3,2048]{1,0:T(4,128)S(1)}, f32[3,2048]{1,0:T(4,128)}, u32[]{:S(2)}) copy-start(f32[3,2048]{1,0:T(4,128)} %src_ref.1) | copy-start | bytes 73732
  43.5 2.5 %collective-permute-start.11 = (bf16[4,16,2048]{2,1,0:T(8,128)(2,1)S(1)}, bf16[4,16,2048]{2,1,0:T(8,128)(2,1)S(1)}, u32[]{:S(2)}, u32[]{:S(2)}) collective-permute-start(bf16[4,16,2048]{2,1,0:T(8,128)(2,1)S(1)} %collective-permute-done.8.refs_3_), channel_id=1, source_target_pairs={{0,16},{16,0},{1,17},{17,1},{2,18},{18,2},{3,19},{19,3},{4,20},{20... | collective-permute-start | bytes 786440 | tf_op jit(solution)/shard_map/ppermute | solution.py:367
  43.5 2.5 %collective-permute-start.12 = (bf16[4,16,2048]{2,1,0:T(8,128)(2,1)S(1)}, bf16[4,16,2048]{2,1,0:T(8,128)(2,1)S(1)}, u32[]{:S(2)}, u32[]{:S(2)}) collective-permute-start(bf16[4,16,2048]{2,1,0:T(8,128)(2,1)S(1)} %collective-permute-done.9.refs_4_.refs_5_), channel_id=1, source_target_pairs={{0,16},{16,0},{1,17},{17,1},{2,18},{18,2},{3,19},{19,3},{4,20},{20... | collective-permute-start | bytes 786440 | tf_op jit(solution)/shard_map/ppermute | solution.py:367
  44.0 2.0 %collective-permute-start.13 = (bf16[4,16,2048]{2,1,0:T(8,128)(2,1)S(1)}, bf16[4,16,2048]{2,1,0:T(8,128)(2,1)S(1)}, u32[]{:S(2)}, u32[]{:S(2)}) collective-permute-start(bf16[4,16,2048]{2,1,0:T(8,128)(2,1)S(1)} %collective-permute-done.10.refs_5_.refs_4_), channel_id=1, source_target_pairs={{0,16},{16,0},{1,17},{17,1},{2,18},{18,2},{3,19},{19,3},{4,20},{20... | collective-permute-start | bytes 786440 | tf_op jit(solution)/shard_map/ppermute | solution.py:367
  48.8 14.8 %collective-permute-start.14 = (f32[128,512]{1,0:T(8,128)S(1)}, f32[128,512]{1,0:T(8,128)S(1)}, u32[]{:S(2)}, u32[]{:S(2)}) collective-permute-start(f32[128,512]{1,0:T(8,128)S(1)} %leaf_sums.5), channel_id=1, source_target_pairs={{0,1},{1,2},{2,3},{3,0},{4,5},{5,6},{6,7},{7,4},{8,9},{9,10},{10,1... | collective-permute-start | bytes 786440 | tf_op jit(solution)/shard_map/ppermute | solution.py:363
  53.2 10.8 %collective-permute-start.15 = (f32[128,512]{1,0:T(8,128)S(1)}, f32[128,512]{1,0:T(8,128)S(1)}, u32[]{:S(2)}, u32[]{:S(2)}) collective-permute-start(f32[128,512]{1,0:T(8,128)S(1)} %leaf_sums.6), channel_id=1, source_target_pairs={{0,2},{1,3},{2,0},{3,1},{4,6},{5,7},{6,4},{7,5},{8,10},{9,11},{10,... | collective-permute-start | bytes 786440 | tf_op jit(solution)/shard_map/ppermute | solution.py:363
  56.9 11.9 %collective-permute-start.16 = (f32[128,512]{1,0:T(8,128)S(1)}, f32[128,512]{1,0:T(8,128)S(1)}, u32[]{:S(2)}, u32[]{:S(2)}) collective-permute-start(f32[128,512]{1,0:T(8,128)S(1)} %leaf_sums.7), channel_id=1, source_target_pairs={{0,3},{1,0},{2,1},{3,2},{4,7},{5,4},{6,5},{7,6},{8,11},{9,8},{10,9... | collective-permute-start | bytes 786440 | tf_op jit(solution)/shard_map/ppermute | solution.py:363
  72.7 4.4 %collective-permute-start.17 = (f32[128,128]{1,0:T(8,128)S(1)}, f32[128,128]{1,0:T(8,128)S(1)}, u32[]{:S(2)}, u32[]{:S(2)}) collective-permute-start(f32[128,128]{1,0:T(8,128)S(1)} %get-tuple-element.30.a_ref), channel_id=1, source_target_pairs={{0,1},{1,0},{2,3},{3,2},{4,5},{5,4},{6,7},{7,6},{8,9},{9,8},{10,11... | collective-permute-start | bytes 196616 | tf_op jit(solution)/shard_map/ppermute | solution.py:367
  80.3 5.9 %collective-permute-start.18 = (f32[128,128]{1,0:T(8,128)S(1)}, f32[128,128]{1,0:T(8,128)S(1)}, u32[]{:S(2)}, u32[]{:S(2)}) collective-permute-start(f32[128,128]{1,0:T(8,128)S(1)} %get-tuple-element.33.a_ref), channel_id=1, source_target_pairs={{0,2},{1,3},{2,0},{3,1},{4,6},{5,7},{6,4},{7,5},{8,10},{9,11},{10,... | collective-permute-start | bytes 196616 | tf_op jit(solution)/shard_map/ppermute | solution.py:367

commit v3 on v2

--- a/solution.py
+++ b/solution.py
@@ -196,62 +196,69 @@
     return (inv, (a * inv) * rest), (inv * inv, a * (rest * rest))
 
 
-def eliminate(gram, aug_ref, top_ref):
+def one_round(at, aug_ref, top_ref):
+    n = 128
+    sub = lax.broadcasted_iota(jnp.int32, (8, n), 0)
+    lane = lax.broadcasted_iota(jnp.int32, (8, n), 1)
+    high = [aug_ref[at:at + 8, :n], aug_ref[at:at + 8, n:]]
+    low = [aug_ref[at + 8:at + 16, :n], aug_ref[at + 8:at + 16, n:]]
+    upper = [spread(high[0], at + k) for k in range(8)]
+    under = [spread(low[0], at + k) for k in range(8)]
+    lower = [spread(low[0], at + 8 + k) for k in range(8)]
+    scale_high = scale_low = jnp.zeros((8, n), F32)
+    for k in range(0, 8, 2):
+        scales, squares = pivots(upper, k)
+        scale_high = jnp.where(sub == k, scales[0], jnp.where(sub == k + 1, scales[1], scale_high))
+        for p, square in ((k, squares[0]), (k + 1, squares[1])):
+            mult = jnp.where(sub > p, upper[p] * square, 0.0)
+            wide = under[p] * square
+            for q in range(p + 1, 8):
+                entry = row(upper[p], q)
+                upper[q] = upper[q] - mult * entry
+                under[q] = under[q] - wide * entry
+            for q in range(8):
+                lower[q] = lower[q] - wide * row(under[p], q)
+            for h in range(2):
+                line = row(high[h], p)
+                low[h] = low[h] - wide * line
+                if p < 7:
+                    high[h] = high[h] - mult * line
+    for k in range(0, 8, 2):
+        scales, squares = pivots(lower, k)
+        scale_low = jnp.where(sub == k, scales[0], jnp.where(sub == k + 1, scales[1], scale_low))
+        for p, square in ((k, squares[0]), (k + 1, squares[1])):
+            if p < 7:
+                mult = jnp.where(sub > p, lower[p] * square, 0.0)
+                for q in range(p + 1, 8):
+                    lower[q] = lower[q] - mult * row(lower[p], q)
+                for h in range(2):
+                    low[h] = low[h] - mult * row(low[h], p)
+    left = [jnp.where(lane >= sub + at, high[0] * scale_high, 0.0), jnp.where(lane >= sub + at + 8, low[0] * scale_low, 0.0)]
+    right = [high[1] * scale_high, low[1] * scale_low]
+    for h in range(2):
+        top_ref[at + 8 * h:at + 8 * h + 8, :n] = left[h]
+        top_ref[at + 8 * h:at + 8 * h + 8, n:] = right[h]
+    if at < n - 16:
+        l1, l2, l3 = parts3(jnp.concatenate(left, axis=0))
+        r1, r2, r3 = parts3(jnp.concatenate(right, axis=0))
+        lhs = jnp.concatenate([l1, l1, l2, l1, l2, l3], axis=0).astype(BF)
+        rl = jnp.concatenate([l1, l2, l1, l3, l2, l1], axis=0)
+        rr = jnp.concatenate([r1, r2, r1, r3, r2, r1], axis=0)
+        rhs = jnp.concatenate([rl, rr], axis=1).astype(BF)
+        upd = lax.dot_general(lhs, rhs, (((0,), (0,)), ((), ())), preferred_element_type=F32)
+        aug_ref[at + 16:, :] -= upd[at + 16:, :]
+
+
+def eliminate(grams, augs, tops):
     n = 128
     i = lax.broadcasted_iota(jnp.int32, (n, n), 0)
     j = lax.broadcasted_iota(jnp.int32, (n, n), 1)
-    aug_ref[:, :n] = gram
-    aug_ref[:, n:] = jnp.where(i == j, 1.0, 0.0)
-    sub = lax.broadcasted_iota(jnp.int32, (8, n), 0)
-    lane = lax.broadcasted_iota(jnp.int32, (8, n), 1)
+    for gram, aug_ref in zip(grams, augs):
+        aug_ref[:, :n] = gram
+        aug_ref[:, n:] = jnp.where(i == j, 1.0, 0.0)
     for at in range(0, n, 16):
-        high = [aug_ref[at:at + 8, :n], aug_ref[at:at + 8, n:]]
-        low = [aug_ref[at + 8:at + 16, :n], aug_ref[at + 8:at + 16, n:]]
-        upper = [spread(high[0], at + k) for k in range(8)]
-        under = [spread(low[0], at + k) for k in range(8)]
-        lower = [spread(low[0], at + 8 + k) for k in range(8)]
-        scale_high = scale_low = jnp.zeros((8, n), F32)
-        for k in range(0, 8, 2):
-            scales, squares = pivots(upper, k)
-            scale_high = jnp.where(sub == k, scales[0], jnp.where(sub == k + 1, scales[1], scale_high))
-            for p, square in ((k, squares[0]), (k + 1, squares[1])):
-                mult = jnp.where(sub > p, upper[p] * square, 0.0)
-                wide = under[p] * square
-                for q in range(p + 1, 8):
-                    entry = row(upper[p], q)
-                    upper[q] = upper[q] - mult * entry
-                    under[q] = under[q] - wide * entry
-                for q in range(8):
-                    lower[q] = lower[q] - wide * row(under[p], q)
-                for h in range(2):
-                    line = row(high[h], p)
-                    low[h] = low[h] - wide * line
-                    if p < 7:
-                        high[h] = high[h] - mult * line
-        for k in range(0, 8, 2):
-            scales, squares = pivots(lower, k)
-            scale_low = jnp.where(sub == k, scales[0], jnp.where(sub == k + 1, scales[1], scale_low))
-            for p, square in ((k, squares[0]), (k + 1, squares[1])):
-                if p < 7:
-                    mult = jnp.where(sub > p, lower[p] * square, 0.0)
-                    for q in range(p + 1, 8):
-                        lower[q] = lower[q] - mult * row(lower[p], q)
-                    for h in range(2):
-                        low[h] = low[h] - mult * row(low[h], p)
-        left = [jnp.where(lane >= sub + at, high[0] * scale_high, 0.0), jnp.where(lane >= sub + at + 8, low[0] * scale_low, 0.0)]
-        right = [high[1] * scale_high, low[1] * scale_low]
-        for h in range(2):
-            top_ref[at + 8 * h:at + 8 * h + 8, :n] = left[h]
-            top_ref[at + 8 * h:at + 8 * h + 8, n:] = right[h]
-        if at < n - 16:
-            l1, l2, l3 = parts3(jnp.concatenate(left, axis=0))
-            r1, r2, r3 = parts3(jnp.concatenate(right, axis=0))
-            lhs = jnp.concatenate([l1, l1, l2, l1, l2, l3], axis=0).astype(BF)
-            rl = jnp.concatenate([l1, l2, l1, l3, l2, l1], axis=0)
-            rr = jnp.concatenate([r1, r2, r1, r3, r2, r1], axis=0)
-            rhs = jnp.concatenate([rl, rr], axis=1).astype(BF)
-            upd = lax.dot_general(lhs, rhs, (((0,), (0,)), ((), ())), preferred_element_type=F32)
-            aug_ref[at + 16:, :] -= upd[at + 16:, :]
+        for aug_ref, top_ref in zip(augs, tops):
+            one_round(at, aug_ref, top_ref)
 
 
 def regular(gram):
@@ -262,12 +269,14 @@
     return gram / mean + jnp.where(i == j, ridge, 0.0), mean
 
 
-def factors(gram, aug_ref, top_ref):
-    scaled, mean = regular(gram)
-    eliminate(scaled, aug_ref, top_ref)
-    inv = top_ref[:, 128:]
-    root = lax.rsqrt(mean)
-    return inv * root, (top_ref[:, :128] - ridge * inv) * (mean * root)
+def factors(grams, augs, tops):
+    scaled, means = zip(*[regular(gram) for gram in grams])
+    eliminate(scaled, augs, tops)
+    found = []
+    for mean, top_ref in zip(means, tops):
+        inv, root = top_ref[:, 128:], lax.rsqrt(mean)
+        found.append((inv * root, (top_ref[:, :128] - ridge * inv) * (mean * root)))
+    return found
 
 
 def tdot(a, b):
@@ -291,14 +300,7 @@
             both = (a_ref[rows, :] + b_ref[rows, :]) + (c_ref[rows, :] + d_ref[rows, :])
             z_ref[pl.ds(pl.multiple_of(plane * 16, 16), 16), :] = both
     z = z_ref[...]
-    inv, proj = factors(ndot(z, z) * (1.0 / LEAF), aug_ref, top_ref)
-    inv_ref[...] = inv
-    proj_ref[...] = proj
-    sq_ref[...] = tdot(proj, proj)
-
-
-def node_body(a_ref, b_ref, inv_ref, proj_ref, sq_ref, aug_ref, top_ref):
-    inv, proj = factors((a_ref[...] + b_ref[...]) * (1.0 / 256), aug_ref, top_ref)
+    ((inv, proj),) = factors([ndot(z, z) * (1.0 / LEAF)], [aug_ref], [top_ref])
     inv_ref[...] = inv
     proj_ref[...] = proj
     sq_ref[...] = tdot(proj, proj)
@@ -310,13 +312,14 @@
     next_ref[...] = mdot(base, proj_ref[...])
 
 
-def carry2_body(z_ref, inv_ref, proj_ref, next_ref):
-    next_ref[...] = mdot(ndot(z_ref[...], inv_ref[...]), proj_ref[...])
-
-
-def last_body(a_ref, b_ref, z_ref, out_ref, aug_ref, top_ref):
-    inv, _ = factors((a_ref[...] + b_ref[...]) * (1.0 / 256), aug_ref, top_ref)
-    out_ref[...] = ndot(z_ref[...], inv) * (1.0 / 128)
+def group_body(own_ref, beside_ref, over_ref, last_ref, z_ref, out_ref, *scratch):
+    augs, tops = scratch[:2], scratch[2:]
+    (inv, proj), (_, other) = factors(
+        [(own_ref[...] + beside_ref[...]) * (1.0 / 256), (over_ref[...] + last_ref[...]) * (1.0 / 256)], augs, tops)
+    both = tdot(proj, proj) + tdot(other, other)
+    carried = mdot(ndot(z_ref[...], inv), proj)
+    ((top_inv, _),) = factors([both * (1.0 / 256)], augs[:1], tops[:1])
+    out_ref[...] = ndot(carried, top_inv) * (1.0 / 128)
 
 
 def sds(*shape):
@@ -338,20 +341,12 @@
     )(*parts)
 
 
-def pair_node(a, b):
-    return pl.pallas_call(node_body, out_shape=(sds(128, 128),) * 3, scratch_shapes=SCR, name="pair_node", compiler_params=params())(a, b)
-
-
 def carry(z, inv, proj):
     return pl.pallas_call(carry_body, out_shape=(sds(512, 128),) * 2, name="carry", compiler_params=params())(z, inv, proj)
 
 
-def carry2(z, inv, proj):
-    return pl.pallas_call(carry2_body, out_shape=sds(512, 128), name="carry2", compiler_params=params())(z, inv, proj)
-
-
-def last_node(a, b, z):
-    return pl.pallas_call(last_body, out_shape=sds(512, 128), scratch_shapes=SCR, name="last_node", compiler_params=params())(a, b, z)
+def group_node(squares, z):
+    return pl.pallas_call(group_body, out_shape=sds(512, 128), scratch_shapes=SCR * 2, name="group_node", compiler_params=params())(*squares, z)
 
 
 ROW = ("z", "c")
@@ -413,12 +408,9 @@
         part = leaf_sums(d, near, targets, base, made, fused, mine, other)
         sums[d] = moved(part, "y", d) if d else part
     far_sample, inv0, proj0, sq0 = leaf_node([sums[d] for d in range(4)])
-    sib = crossed(sq0, "y", 1)
+    squares = [sq0] + [crossed(sq0, "y", k) for k in (1, 2, 3)]
     leaf_basis, carried = carry(far_sample, inv0, proj0)
-    inv1, proj1, sq1 = pair_node(sq0, after(sib, carried))
-    cousin = crossed(sq1, "y", 2)
-    carried = carry2(carried, inv1, proj1)
-    nested = last_node(sq1, cousin, carried)
+    nested = group_node(squares[:2] + [after(sq, carried) for sq in squares[2:]], carried)
     return (leaf_basis, nested)
 
 

time: 90.6 us -> 89 us (0.982); the launches traced: 90.3 us -> 87.5 us
  waiting for transfers between devices: 13.6 us -> 7.85 us
  starting transfers between devices: 27.4 us -> 31 us
    ppermute x12 -> x13, waiting for transfers between devices: 8.33 us -> 2.58 us  [crossed(): lax.ppermute(x, axis, [(i, i ^ bit) for i in range(lax.axis_size(axis))])]
    ppermute x12 -> x13, starting transfers between devices: 11.2 us -> 14.8 us  [crossed(): lax.ppermute(x, axis, [(i, i ^ bit) for i in range(lax.axis_size(axis))])]
    pallas_call x3 -> x1, Pallas kernels: 8.39 us -> 7.8 us  [group_node(): pl.pallas_call(group_body, out_shape=sds(512, 128), scratch_shapes=SCR *...]
  transfers between devices with their start and end apart: 19 -> 20, of which waited for: 5 -> 5; matrix products, arithmetic and copies ran while one was open for 2% -> 2% of each run, Pallas kernels for 34% -> 34%
where the time goes in v3:
time: 89 us; the launch traced here: 87.5 us
  Pallas kernels  44.5 us (50%)
  starting transfers between devices  31 us (35%)
  waiting for transfers between devices  7.85 us (9%)
  other arithmetic  1.69 us (2%)
  local copies, waits for them, and re-layouts  1.61 us (2%)
    ppermute x13, starting transfers between devices, crossed(): lax.ppermute(x, axis, [(i, i ^ bit) for i in range(lax.axis_size(axis))])  14.8 us
    pallas_call x4, Pallas kernels, leaf_sums(): pl.pallas_call(functools.partial(sums_body, turn, stored, fused, [tiles[q...  12.1 us
    pallas_call x3, Pallas kernels, kernel_tiles(): pl.pallas_call(functools.partial(tiles_body, q, first, end), out_shape=ja...  11.7 us
    ppermute x4, starting transfers between devices, over_planes(): return lax.ppermute(x, ROW, pairs)  10.8 us
    pallas_call x1, Pallas kernels, group_node(): pl.pallas_call(group_body, out_shape=sds(512, 128), scratch_shapes=SCR *...  7.8 us
    pallas_call x1, Pallas kernels, own_sums(): pl.pallas_call(own_body, out_shape=jax.ShapeDtypeStruct((4, 128, LEAF), F...  7.75 us
    ppermute x3, starting transfers between devices, moved(): return lax.ppermute(x, axis, [(i, (i + by) % size) for i in range(size)])  5.38 us
    ppermute x3, waiting for transfers between devices, moved(): return lax.ppermute(x, axis, [(i, (i + by) % size) for i in range(size)])  5.26 us
  transfers between devices with their start and end apart: 20, of which 5 were waited for; matrix products, arithmetic and copies ran while one was open for 2% of the time, Pallas kernels for 34%

profile of v3, /device:TPU:8, one launch (start us, length us, event | category | flops | bytes accessed | tf_op | source)
XLA Modules:
  0.0 87.5 jit_solution(5043698689457069163)
XLA Ops:
  0.7 1.6 %collective-permute-start.5 = (f32[3,2048]{1,0:T(4,128)}, f32[3,2048]{1,0:T(4,128)S(1)}, u32[]{:S(2)}, u32[]{:S(2)}) collective-permute-start(f32[3,2048]{1,0:T(4,128)} %src_ref.1), channel_id=1, source_target_pairs={{0,4},{4,0},{8,12},{12,8},{1,5},{5,1},{9,13},{13,9},{2,6},{6,2},{1... | collective-permute-start | bytes 73736 | tf_op jit(solution)/shard_map/ppermute | solution.py:362
  2.3 0.8 maximum_select_fusion
  3.2 6.4 %collective-permute-start.4 = (bf16[16,2048]{1,0:T(8,128)(2,1)S(1)}, bf16[16,2048]{1,0:T(8,128)(2,1)S(1)}, u32[]{:S(2)}, u32[]{:S(2)}) collective-permute-start(bf16[16,2048]{1,0:T(8,128)(2,1)S(1)} %maximum_select_fusion), channel_id=1, source_target_pairs={{0,192},{16,240},{32,224},{48,16},{64,0},{80,48},{96,32},{112,80},... | collective-permute-start | bytes 196616 | tf_op jit(solution)/shard_map/ppermute | solution.py:367
  9.5 1.0 %collective-permute-start.3 = (bf16[16,2048]{1,0:T(8,128)(2,1)S(1)}, bf16[16,2048]{1,0:T(8,128)(2,1)S(1)}, u32[]{:S(2)}, u32[]{:S(2)}) collective-permute-start(bf16[16,2048]{1,0:T(8,128)(2,1)S(1)} %maximum_select_fusion), channel_id=1, source_target_pairs={{0,128},{16,176},{32,160},{48,208},{64,192},{80,240},{96,224},{112... | collective-permute-start | bytes 196616 | tf_op jit(solution)/shard_map/ppermute | solution.py:367
  10.5 2.8 %collective-permute-start.2 = (bf16[16,2048]{1,0:T(8,128)(2,1)S(1)}, bf16[16,2048]{1,0:T(8,128)(2,1)S(1)}, u32[]{:S(2)}, u32[]{:S(2)}) collective-permute-start(bf16[16,2048]{1,0:T(8,128)(2,1)S(1)} %maximum_select_fusion), channel_id=1, source_target_pairs={{0,64},{16,112},{32,96},{48,144},{64,128},{80,176},{96,160},{112,2... | collective-permute-start | bytes 196616 | tf_op jit(solution)/shard_map/ppermute | solution.py:367
  13.4 0.7 collective-permute-start.1
  14.0 0.8 pad_maximum_fusion.1
  14.8 2.9 %collective-permute-start.7 = (f32[2,3,2048]{2,1,0:T(4,128)S(1)}, f32[2,3,2048]{2,1,0:T(4,128)S(1)}, u32[]{:S(2)}, u32[]{:S(2)}) collective-permute-start(f32[2,3,2048]{2,1,0:T(4,128)S(1)} %pad_maximum_fusion.1), channel_id=1, source_target_pairs={{0,8},{4,12},{8,0},{12,4},{1,9},{5,13},{9,1},{13,5},{2,10},{6,14},... | collective-permute-start | bytes 147464 | tf_op jit(solution)/shard_map/ppermute | solution.py:362
  17.7 0.9 %copy-done = f32[3,8192]{1,0:T(4,128)S(1)} copy-done((f32[3,8192]{1,0:T(4,128)S(1)}, f32[3,8192]{1,0:T(4,128)}, u32[]{:S(2)}) %copy-start) | copy-done | bytes 98328
  18.6 0.7 copy-done.2
  19.3 6.2 %kernel_tiles.3.refs_0_ = bf16[4,2048,512]{2,1,0:T(8,128)(2,1)S(1)} custom-call(s32[8,16]{1,0:T(8,128)S(1)} %bitcast.15, f32[3,8192]{1,0:T(4,128)S(1)} %copy-done, f32[3,2048]{1,0:T(4,128)S(1)} %collective-permute-done.5.src_ref), custom_call_target="tpu_custom_call" | custom-call | flops 8000000000 | bytes 8400000 | tf_op jit(solution)/shard_map/kernel_tiles/pallas_call | solution.py:90
  25.9 0.7 collective-permute-start.8
  26.5 2.0 %collective-permute-start.9 = (bf16[4,16,2048]{2,1,0:T(8,128)(2,1)S(1)}, bf16[4,16,2048]{2,1,0:T(8,128)(2,1)S(1)}, u32[]{:S(2)}, u32[]{:S(2)}) collective-permute-start(bf16[4,16,2048]{2,1,0:T(8,128)(2,1)S(1)} %pad_maximum_fusion.mine_ref), channel_id=1, source_target_pairs={{0,8},{4,12},{8,0},{12,4},{1,9},{5,13},{9,1},{13,5},{2,10},{6,14},... | collective-permute-start | bytes 786440 | tf_op jit(solution)/shard_map/ppermute | solution.py:362
  28.5 2.1 %collective-permute-start.10 = (bf16[4,16,2048]{2,1,0:T(8,128)(2,1)S(1)}, bf16[4,16,2048]{2,1,0:T(8,128)(2,1)S(1)}, u32[]{:S(2)}, u32[]{:S(2)}) collective-permute-start(bf16[4,16,2048]{2,1,0:T(8,128)(2,1)S(1)} %pad_maximum_fusion.mine_ref), channel_id=1, source_target_pairs={{0,12},{4,8},{8,4},{12,0},{1,13},{5,9},{9,5},{13,1},{2,14},{6,10},... | collective-permute-start | bytes 786440 | tf_op jit(solution)/shard_map/ppermute | solution.py:362
  30.6 3.4 %kernel_tiles.4.refs_1_ = bf16[2,2048,512]{2,1,0:T(8,128)(2,1)S(1)} custom-call(s32[8,16]{1,0:T(8,128)S(1)} %bitcast.16, f32[3,8192]{1,0:T(4,128)S(1)} %copy-done, f32[3,2048]{1,0:T(4,128)S(1)} %get-tuple-element.19.src_ref.refs_2_), custom_call_target="tpu_custom_call" | custom-call | flops 8000000000 | bytes 8400000 | tf_op jit(solution)/shard_map/kernel_tiles/pallas_call | solution.py:90
  34.1 7.8 %own_sums.1.base_ref = f32[4,128,512]{2,1,0:T(8,128)S(1)} custom-call(s32[8,16]{1,0:T(8,128)S(1)} %bitcast.17, f32[3,8192]{1,0:T(4,128)S(1)} %copy-done, f32[3,2048]{1,0:T(4,128)S(1)} %copy-done.1, bf16[4,16,2048]{2,1,0:T(8,128)(2,1)S(1)} %pad_maximum_fusion.mine_ref, bf16[4,16,2048]{2,1,0:T(8,128)(2,1)S(1)} %collective-permute-done.6.other_ref), custom_call_target="tpu_custom_call" | custom-call | flops 8000000000 | bytes 8400000 | tf_op jit(solution)/shard_map/own_sums/pallas_call | solution.py:126
  41.9 1.6 %collective-permute-done.10.refs_5_.refs_4_ = bf16[4,16,2048]{2,1,0:T(8,128)(2,1)S(1)} collective-permute-done((bf16[4,16,2048]{2,1,0:T(8,128)(2,1)S(1)}, bf16[4,16,2048]{2,1,0:T(8,128)(2,1)S(1)}, u32[]{:S(2)}, u32[]{:S(2)}) %collective-permute-start.10) | collective-permute-done | bytes 262176 | tf_op jit(solution)/shard_map/ppermute | solution.py:362
  44.0 2.0 %kernel_tiles.5.refs_1_ = bf16[1,2048,512]{2,1,0:T(8,128)(2,1)S(1)} custom-call(s32[8,16]{1,0:T(8,128)S(1)} %bitcast.18, f32[3,8192]{1,0:T(4,128)S(1)} %copy-done, f32[3,2048]{1,0:T(4,128)S(1)} %get-tuple-element.19.src_ref.refs_2_), custom_call_target="tpu_custom_call" | custom-call | flops 8000000000 | bytes 8400000 | tf_op jit(solution)/shard_map/kernel_tiles/pallas_call | solution.py:90
  46.1 2.7 %leaf_sums.5 = f32[128,512]{1,0:T(8,128)S(1)} custom-call(s32[8,16]{1,0:T(8,128)S(1)} %bitcast.19, f32[3,8192]{1,0:T(4,128)S(1)} %copy-done, f32[4,128,512]{2,1,0:T(8,128)S(1)} %own_sums.1.base_ref, bf16[4,2048,512]{2,1,0:T(8,128)(2,1)S(1)} %kernel_tiles.3.refs_0_, bf16[2,2048,512]{2,1,0:T(8,128)(2,1)S(1)} %kernel_tiles.4.refs_1_, ...), custom_call_target="tpu_custom_call" | custom-call | flops 4000000000 | bytes 9000000 | tf_op jit(solution)/shard_map/leaf_sums/pallas_call | solution.py:168
  48.8 1.6 %collective-permute-start.14 = (f32[128,512]{1,0:T(8,128)S(1)}, f32[128,512]{1,0:T(8,128)S(1)}, u32[]{:S(2)}, u32[]{:S(2)}) collective-permute-start(f32[128,512]{1,0:T(8,128)S(1)} %leaf_sums.5), channel_id=1, source_target_pairs={{0,1},{1,2},{2,3},{3,0},{4,5},{5,6},{6,7},{7,4},{8,9},{9,10},{10,1... | collective-permute-start | bytes 786440 | tf_op jit(solution)/shard_map/ppermute | solution.py:358
  50.4 2.7 %leaf_sums.6 = f32[128,512]{1,0:T(8,128)S(1)} custom-call(s32[8,16]{1,0:T(8,128)S(1)} %bitcast.20, f32[3,8192]{1,0:T(4,128)S(1)} %copy-done, f32[4,128,512]{2,1,0:T(8,128)S(1)} %own_sums.1.base_ref, bf16[4,2048,512]{2,1,0:T(8,128)(2,1)S(1)} %kernel_tiles.3.refs_0_, bf16[2,2048,512]{2,1,0:T(8,128)(2,1)S(1)} %kernel_tiles.4.refs_1_, ...), custom_call_target="tpu_custom_call" | custom-call | flops 4000000000 | bytes 9000000 | tf_op jit(solution)/shard_map/leaf_sums/pallas_call | solution.py:168
  53.2 1.0 %collective-permute-start.15 = (f32[128,512]{1,0:T(8,128)S(1)}, f32[128,512]{1,0:T(8,128)S(1)}, u32[]{:S(2)}, u32[]{:S(2)}) collective-permute-start(f32[128,512]{1,0:T(8,128)S(1)} %leaf_sums.6), channel_id=1, source_target_pairs={{0,2},{1,3},{2,0},{3,1},{4,6},{5,7},{6,4},{7,5},{8,10},{9,11},{10,... | collective-permute-start | bytes 786440 | tf_op jit(solution)/shard_map/ppermute | solution.py:358
  54.2 2.7 %leaf_sums.7 = f32[128,512]{1,0:T(8,128)S(1)} custom-call(s32[8,16]{1,0:T(8,128)S(1)} %bitcast.21, f32[3,8192]{1,0:T(4,128)S(1)} %copy-done, f32[4,128,512]{2,1,0:T(8,128)S(1)} %own_sums.1.base_ref, bf16[4,2048,512]{2,1,0:T(8,128)(2,1)S(1)} %kernel_tiles.3.refs_0_, bf16[1,2048,512]{2,1,0:T(8,128)(2,1)S(1)} %kernel_tiles.5.refs_1_, ...), custom_call_target="tpu_custom_call" | custom-call | flops 4000000000 | bytes 9000000 | tf_op jit(solution)/shard_map/leaf_sums/pallas_call | solution.py:168
  56.9 2.7 %collective-permute-start.16 = (f32[128,512]{1,0:T(8,128)S(1)}, f32[128,512]{1,0:T(8,128)S(1)}, u32[]{:S(2)}, u32[]{:S(2)}) collective-permute-start(f32[128,512]{1,0:T(8,128)S(1)} %leaf_sums.7), channel_id=1, source_target_pairs={{0,3},{1,0},{2,1},{3,2},{4,7},{5,4},{6,5},{7,6},{8,11},{9,8},{10,9... | collective-permute-start | bytes 786440 | tf_op jit(solution)/shard_map/ppermute | solution.py:358
  59.6 3.9 %leaf_sums.4.a_ref = f32[128,512]{1,0:T(8,128)S(1)} custom-call(s32[8,16]{1,0:T(8,128)S(1)} %bitcast.22, f32[3,8192]{1,0:T(4,128)S(1)} %copy-done, f32[4,128,512]{2,1,0:T(8,128)S(1)} %own_sums.1.base_ref, bf16[4,2048,512]{2,1,0:T(8,128)(2,1)S(1)} %kernel_tiles.3.refs_0_, f32[3,2048]{1,0:T(4,128)S(1)} %get-tuple-element.32.refs_1_.refs_2_, ...), custom_call_target="tpu_custom_call" | custom-call | flops 4000000000 | bytes 9000000 | tf_op jit(solution)/shard_map/leaf_sums/pallas_call | solution.py:168
  64.0 4.8 %collective-permute-done.16.d_ref = f32[128,512]{1,0:T(8,128)S(1)} collective-permute-done((f32[128,512]{1,0:T(8,128)S(1)}, f32[128,512]{1,0:T(8,128)S(1)}, u32[]{:S(2)}, u32[]{:S(2)}) %collective-permute-start.16) | collective-permute-done | bytes 262176 | tf_op jit(solution)/shard_map/ppermute | solution.py:358
  68.8 3.9 %leaf_node.1 = (f32[128,512]{1,0:T(8,128)S(1)}, f32[128,128]{1,0:T(8,128)S(1)}, f32[128,128]{1,0:T(8,128)S(1)}, f32[128,128]{1,0:T(8,128)S(1)}) custom-call(f32[128,512]{1,0:T(8,128)S(1)} %leaf_sums.4.a_ref, f32[128,512]{1,0:T(8,128)S(1)} %collective-permute-done.14.b_ref, f32[128,512]{1,0:T(8,128)S(1)} %collective-permute-done.15.c_ref, ...), custom_call_target="tpu_custom_call" | custom-call | tf_op jit(solution)/shard_map/leaf_node/pallas_call | solution.py:334
  72.7 1.1 %collective-permute-start.18 = (f32[128,128]{1,0:T(8,128)S(1)}, f32[128,128]{1,0:T(8,128)S(1)}, u32[]{:S(2)}, u32[]{:S(2)}) collective-permute-start(f32[128,128]{1,0:T(8,128)S(1)} %get-tuple-element.28.own_ref), channel_id=1, source_target_pairs={{0,2},{1,3},{2,0},{3,1},{4,6},{5,7},{6,4},{7,5},{8,10},{9,11},{10,... | collective-permute-start | bytes 196616 | tf_op jit(solution)/shard_map/ppermute | solution.py:362
  73.8 3.7 %collective-permute-start.17 = (f32[128,128]{1,0:T(8,128)S(1)}, f32[128,128]{1,0:T(8,128)S(1)}, u32[]{:S(2)}, u32[]{:S(2)}) collective-permute-start(f32[128,128]{1,0:T(8,128)S(1)} %get-tuple-element.28.own_ref), channel_id=1, source_target_pairs={{0,1},{1,0},{2,3},{3,2},{4,5},{5,4},{6,7},{7,6},{8,9},{9,8},{10,11... | collective-permute-start | bytes 196616 | tf_op jit(solution)/shard_map/ppermute | solution.py:362
  77.5 1.3 %carry.1 = (f32[512,128]{1,0:T(8,128)}, f32[512,128]{1,0:T(8,128)S(1)}) custom-call(f32[128,512]{1,0:T(8,128)S(1)} %get-tuple-element.24.z_ref, f32[128,128]{1,0:T(8,128)S(1)} %get-tuple-element.25.inv_ref, f32[128,128]{1,0:T(8,128)S(1)} %get-tuple-element.26.proj_ref), custom_call_target="tpu_custom_call" | custom-call | tf_op jit(solution)/shard_map/carry/pallas_call | solution.py:345
  79.0 0.7 collective-permute-done.17.beside_ref
  79.7 7.8 %group_node.1 = f32[512,128]{1,0:T(8,128)} custom-call(f32[128,128]{1,0:T(8,128)S(1)} %get-tuple-element.28.own_ref, f32[128,128]{1,0:T(8,128)S(1)} %collective-permute-done.17.beside_ref, f32[128,128]{1,0:T(8,128)S(1)} %collective-permute-done.18.over_ref, f32[128,128]{1,0:T(8,128)S(1)} %collective-permute-done.19.last_ref, ...), custom_call_target="tpu_custom_call" | custom-call | tf_op jit(solution)/shard_map/group_node/pallas_call | solution.py:349
  (32 shorter events, 1.5 us)
Async XLA Ops:
  0.6 1.7 %collective-permute-start = (bf16[8,2048]{1,0:T(8,128)(2,1)}, bf16[8,2048]{1,0:T(8,128)(2,1)S(1)}, u32[]{:S(2)}, u32[]{:S(2)}) collective-permute-start(bf16[8,2048]{1,0:T(8,128)(2,1)} %bitcast.23), channel_id=1, source_target_pairs={{0,16},{16,0},{1,17},{17,1},{2,18},{18,2},{3,19},{19,3},{4,20},{20... | collective-permute-start | bytes 98312 | tf_op jit(solution)/shard_map/ppermute | solution.py:362
  0.7 13.3 %collective-permute-start.5 = (f32[3,2048]{1,0:T(4,128)}, f32[3,2048]{1,0:T(4,128)S(1)}, u32[]{:S(2)}, u32[]{:S(2)}) collective-permute-start(f32[3,2048]{1,0:T(4,128)} %src_ref.1), channel_id=1, source_target_pairs={{0,4},{4,0},{8,12},{12,8},{1,5},{5,1},{9,13},{13,9},{2,6},{6,2},{1... | collective-permute-start | bytes 73736 | tf_op jit(solution)/shard_map/ppermute | solution.py:362
  3.2 22.5 %collective-permute-start.4 = (bf16[16,2048]{1,0:T(8,128)(2,1)S(1)}, bf16[16,2048]{1,0:T(8,128)(2,1)S(1)}, u32[]{:S(2)}, u32[]{:S(2)}) collective-permute-start(bf16[16,2048]{1,0:T(8,128)(2,1)S(1)} %maximum_select_fusion), channel_id=1, source_target_pairs={{0,192},{16,240},{32,224},{48,16},{64,0},{80,48},{96,32},{112,80},... | collective-permute-start | bytes 196616 | tf_op jit(solution)/shard_map/ppermute | solution.py:367
  9.5 16.1 %collective-permute-start.3 = (bf16[16,2048]{1,0:T(8,128)(2,1)S(1)}, bf16[16,2048]{1,0:T(8,128)(2,1)S(1)}, u32[]{:S(2)}, u32[]{:S(2)}) collective-permute-start(bf16[16,2048]{1,0:T(8,128)(2,1)S(1)} %maximum_select_fusion), channel_id=1, source_target_pairs={{0,128},{16,176},{32,160},{48,208},{64,192},{80,240},{96,224},{112... | collective-permute-start | bytes 196616 | tf_op jit(solution)/shard_map/ppermute | solution.py:367
  10.5 15.1 %collective-permute-start.2 = (bf16[16,2048]{1,0:T(8,128)(2,1)S(1)}, bf16[16,2048]{1,0:T(8,128)(2,1)S(1)}, u32[]{:S(2)}, u32[]{:S(2)}) collective-permute-start(bf16[16,2048]{1,0:T(8,128)(2,1)S(1)} %maximum_select_fusion), channel_id=1, source_target_pairs={{0,64},{16,112},{32,96},{48,144},{64,128},{80,176},{96,160},{112,2... | collective-permute-start | bytes 196616 | tf_op jit(solution)/shard_map/ppermute | solution.py:367
  13.4 12.2 %collective-permute-start.1 = (bf16[16,2048]{1,0:T(8,128)(2,1)S(1)}, bf16[16,2048]{1,0:T(8,128)(2,1)S(1)}, u32[]{:S(2)}, u32[]{:S(2)}) collective-permute-start(bf16[16,2048]{1,0:T(8,128)(2,1)S(1)} %maximum_select_fusion), channel_id=1, source_target_pairs={{16,48},{48,80},{80,112},{112,144},{144,176},{176,208},{208,240},{... | collective-permute-start | bytes 196616 | tf_op jit(solution)/shard_map/ppermute | solution.py:367
  14.8 11.0 %collective-permute-start.7 = (f32[2,3,2048]{2,1,0:T(4,128)S(1)}, f32[2,3,2048]{2,1,0:T(4,128)S(1)}, u32[]{:S(2)}, u32[]{:S(2)}) collective-permute-start(f32[2,3,2048]{2,1,0:T(4,128)S(1)} %pad_maximum_fusion.1), channel_id=1, source_target_pairs={{0,8},{4,12},{8,0},{12,4},{1,9},{5,13},{9,1},{13,5},{2,10},{6,14},... | collective-permute-start | bytes 147464 | tf_op jit(solution)/shard_map/ppermute | solution.py:362
  17.7 0.9 %copy-start = (f32[3,8192]{1,0:T(4,128)S(1)}, f32[3,8192]{1,0:T(4,128)}, u32[]{:S(2)}) copy-start(f32[3,8192]{1,0:T(4,128)} %tgt_ref.15) | copy-start | bytes 294916
  18.6 0.7 copy-start.2
  19.3 6.3 %copy-start.3 = (bf16[2048,8]{0,1:T(8,128)(2,1)S(1)}, bf16[2048,8]{0,1:T(8,128)(2,1)}, u32[]{:S(2)}) copy-start(bf16[2048,8]{0,1:T(8,128)(2,1)} %param.6) | copy-start | bytes 98308
  25.7 4.9 %collective-permute-start.6 = (bf16[4,16,2048]{2,1,0:T(8,128)(2,1)S(1)}, bf16[4,16,2048]{2,1,0:T(8,128)(2,1)S(1)}, u32[]{:S(2)}, u32[]{:S(2)}) collective-permute-start(bf16[4,16,2048]{2,1,0:T(8,128)(2,1)S(1)} %pad_maximum_fusion.mine_ref), channel_id=1, source_target_pairs={{0,16},{16,0},{1,17},{17,1},{2,18},{18,2},{3,19},{19,3},{4,20},{20... | collective-permute-start | bytes 786440 | tf_op jit(solution)/shard_map/ppermute | solution.py:362
  25.9 16.0 %collective-permute-start.8 = (bf16[4,16,2048]{2,1,0:T(8,128)(2,1)S(1)}, bf16[4,16,2048]{2,1,0:T(8,128)(2,1)S(1)}, u32[]{:S(2)}, u32[]{:S(2)}) collective-permute-start(bf16[4,16,2048]{2,1,0:T(8,128)(2,1)S(1)} %pad_maximum_fusion.mine_ref), channel_id=1, source_target_pairs={{0,4},{4,0},{8,12},{12,8},{1,5},{5,1},{9,13},{13,9},{2,6},{6,2},{1... | collective-permute-start | bytes 786440 | tf_op jit(solution)/shard_map/ppermute | solution.py:362
  26.5 15.4 %collective-permute-start.9 = (bf16[4,16,2048]{2,1,0:T(8,128)(2,1)S(1)}, bf16[4,16,2048]{2,1,0:T(8,128)(2,1)S(1)}, u32[]{:S(2)}, u32[]{:S(2)}) collective-permute-start(bf16[4,16,2048]{2,1,0:T(8,128)(2,1)S(1)} %pad_maximum_fusion.mine_ref), channel_id=1, source_target_pairs={{0,8},{4,12},{8,0},{12,4},{1,9},{5,13},{9,1},{13,5},{2,10},{6,14},... | collective-permute-start | bytes 786440 | tf_op jit(solution)/shard_map/ppermute | solution.py:362
  28.5 15.0 %collective-permute-start.10 = (bf16[4,16,2048]{2,1,0:T(8,128)(2,1)S(1)}, bf16[4,16,2048]{2,1,0:T(8,128)(2,1)S(1)}, u32[]{:S(2)}, u32[]{:S(2)}) collective-permute-start(bf16[4,16,2048]{2,1,0:T(8,128)(2,1)S(1)} %pad_maximum_fusion.mine_ref), channel_id=1, source_target_pairs={{0,12},{4,8},{8,4},{12,0},{1,13},{5,9},{9,5},{13,1},{2,14},{6,10},... | collective-permute-start | bytes 786440 | tf_op jit(solution)/shard_map/ppermute | solution.py:362
  30.6 3.4 %copy-start.1 = (f32[3,2048]{1,0:T(4,128)S(1)}, f32[3,2048]{1,0:T(4,128)}, u32[]{:S(2)}) copy-start(f32[3,2048]{1,0:T(4,128)} %src_ref.1) | copy-start | bytes 73732
  43.5 2.5 %collective-permute-start.11 = (bf16[4,16,2048]{2,1,0:T(8,128)(2,1)S(1)}, bf16[4,16,2048]{2,1,0:T(8,128)(2,1)S(1)}, u32[]{:S(2)}, u32[]{:S(2)}) collective-permute-start(bf16[4,16,2048]{2,1,0:T(8,128)(2,1)S(1)} %collective-permute-done.8.refs_3_), channel_id=1, source_target_pairs={{0,16},{16,0},{1,17},{17,1},{2,18},{18,2},{3,19},{19,3},{4,20},{20... | collective-permute-start | bytes 786440 | tf_op jit(solution)/shard_map/ppermute | solution.py:362
  43.5 2.5 %collective-permute-start.12 = (bf16[4,16,2048]{2,1,0:T(8,128)(2,1)S(1)}, bf16[4,16,2048]{2,1,0:T(8,128)(2,1)S(1)}, u32[]{:S(2)}, u32[]{:S(2)}) collective-permute-start(bf16[4,16,2048]{2,1,0:T(8,128)(2,1)S(1)} %collective-permute-done.9.refs_4_.refs_5_), channel_id=1, source_target_pairs={{0,16},{16,0},{1,17},{17,1},{2,18},{18,2},{3,19},{19,3},{4,20},{20... | collective-permute-start | bytes 786440 | tf_op jit(solution)/shard_map/ppermute | solution.py:362
  44.0 2.0 %collective-permute-start.13 = (bf16[4,16,2048]{2,1,0:T(8,128)(2,1)S(1)}, bf16[4,16,2048]{2,1,0:T(8,128)(2,1)S(1)}, u32[]{:S(2)}, u32[]{:S(2)}) collective-permute-start(bf16[4,16,2048]{2,1,0:T(8,128)(2,1)S(1)} %collective-permute-done.10.refs_5_.refs_4_), channel_id=1, source_target_pairs={{0,16},{16,0},{1,17},{17,1},{2,18},{18,2},{3,19},{19,3},{4,20},{20... | collective-permute-start | bytes 786440 | tf_op jit(solution)/shard_map/ppermute | solution.py:362
  48.8 14.8 %collective-permute-start.14 = (f32[128,512]{1,0:T(8,128)S(1)}, f32[128,512]{1,0:T(8,128)S(1)}, u32[]{:S(2)}, u32[]{:S(2)}) collective-permute-start(f32[128,512]{1,0:T(8,128)S(1)} %leaf_sums.5), channel_id=1, source_target_pairs={{0,1},{1,2},{2,3},{3,0},{4,5},{5,6},{6,7},{7,4},{8,9},{9,10},{10,1... | collective-permute-start | bytes 786440 | tf_op jit(solution)/shard_map/ppermute | solution.py:358
  53.2 10.8 %collective-permute-start.15 = (f32[128,512]{1,0:T(8,128)S(1)}, f32[128,512]{1,0:T(8,128)S(1)}, u32[]{:S(2)}, u32[]{:S(2)}) collective-permute-start(f32[128,512]{1,0:T(8,128)S(1)} %leaf_sums.6), channel_id=1, source_target_pairs={{0,2},{1,3},{2,0},{3,1},{4,6},{5,7},{6,4},{7,5},{8,10},{9,11},{10,... | collective-permute-start | bytes 786440 | tf_op jit(solution)/shard_map/ppermute | solution.py:358
  56.9 11.9 %collective-permute-start.16 = (f32[128,512]{1,0:T(8,128)S(1)}, f32[128,512]{1,0:T(8,128)S(1)}, u32[]{:S(2)}, u32[]{:S(2)}) collective-permute-start(f32[128,512]{1,0:T(8,128)S(1)} %leaf_sums.7), channel_id=1, source_target_pairs={{0,3},{1,0},{2,1},{3,2},{4,7},{5,4},{6,5},{7,6},{8,11},{9,8},{10,9... | collective-permute-start | bytes 786440 | tf_op jit(solution)/shard_map/ppermute | solution.py:358
  72.7 6.3 %collective-permute-start.18 = (f32[128,128]{1,0:T(8,128)S(1)}, f32[128,128]{1,0:T(8,128)S(1)}, u32[]{:S(2)}, u32[]{:S(2)}) collective-permute-start(f32[128,128]{1,0:T(8,128)S(1)} %get-tuple-element.28.own_ref), channel_id=1, source_target_pairs={{0,2},{1,3},{2,0},{3,1},{4,6},{5,7},{6,4},{7,5},{8,10},{9,11},{10,... | collective-permute-start | bytes 196616 | tf_op jit(solution)/shard_map/ppermute | solution.py:362
  73.8 5.2 %collective-permute-start.19 = (f32[128,128]{1,0:T(8,128)S(1)}, f32[128,128]{1,0:T(8,128)S(1)}, u32[]{:S(2)}, u32[]{:S(2)}) collective-permute-start(f32[128,128]{1,0:T(8,128)S(1)} %get-tuple-element.28.own_ref), channel_id=1, source_target_pairs={{0,3},{1,2},{2,1},{3,0},{4,7},{5,6},{6,5},{7,4},{8,11},{9,10},{10,... | collective-permute-start | bytes 196616 | tf_op jit(solution)/shard_map/ppermute | solution.py:362
  73.8 5.9 %collective-permute-start.17 = (f32[128,128]{1,0:T(8,128)S(1)}, f32[128,128]{1,0:T(8,128)S(1)}, u32[]{:S(2)}, u32[]{:S(2)}) collective-permute-start(f32[128,128]{1,0:T(8,128)S(1)} %get-tuple-element.28.own_ref), channel_id=1, source_target_pairs={{0,1},{1,0},{2,3},{3,2},{4,5},{5,4},{6,7},{7,6},{8,9},{9,8},{10,11... | collective-permute-start | bytes 196616 | tf_op jit(solution)/shard_map/ppermute | solution.py:362
